TPU v7x, 256 devices: a whole 4x4x8 slice. The times are simulated.
256 devices in a mesh: tm: 256 (over y, z, x, core).
Axes of the slice: x: 4, y: 4, z: 8, core: 2. Of those that a mesh axis runs over, the one named last changes fastest.
Arguments:
- step_ops: float32 [512, 256, 256], P('tm')
- sources: float32 [512, 256], P('tm'), may hold values from -0.3 to 0.3
- terminal: float32 [256], replicated, may hold values from -6 to 6
- inertia_jac: float32 [512, 64], P('tm')
- gen_bus: int32 [64], replicated, may hold values from 0 to 255, as said below
Outputs:
- adjoint_states: float32 [512, 256], P('tm')
- sensitivity: float32 [64], replicated
Inputs may be any that keep to these rules, and one draw needn't show every extreme that they name: `gen_bus`: the 64 entries are distinct state indices.
All inputs are finite; a program needn't handle non-finite values.
Results may differ from a plain program's by a relative error of at most 0.0003.
Values sent between devices are 32-bit elements; how exact they have to be, the bound alone decides.
No kernel may reach another device: no remote copies, remote signals or barrier semaphores. Data moves between devices by JAX's collectives and lax.ppermute only.
A program may use at most 256 MiB of HBM per device.

v0:
```python
import jax
import jax.numpy as jnp
from jax import lax
from jax.sharding import PartitionSpec as P


def prefix_2(value, axis, join, neutral):
    count, mine = (lax.axis_size(axis), lax.axis_index(axis))
    pieces = jax.tree.map(lambda part: lax.all_gather(part, axis), value)
    pieces = jax.tree.map(lambda part: part[::-1], pieces)
    mine = count - 1 - mine
    running = jax.tree.map(
        lambda part, zero: jnp.full_like(part, 0) + jnp.asarray(zero, part.dtype), value, neutral
    )

    def turn(position, running):
        longer = join(running, jax.tree.map(lambda part: part[position], pieces))
        return jax.tree.map(lambda new, old: jnp.where(position < mine, new, old), longer, running)

    return lax.fori_loop(0, count - 1, turn, running)


def matmul(left, right):
    return jnp.dot(left, right, precision=lax.Precision.HIGHEST, preferred_element_type=jnp.float32)


def combine(earlier, later):
    return (matmul(later[0], earlier[0]), matmul(later[0], earlier[1]) + later[1])


def on_device(step_ops, sources, terminal, inertia_jac, gen_bus):
    steps_here = step_ops.shape[0]
    width = step_ops.shape[1]
    block_map = step_ops[steps_here - 1]
    block_vec = sources[steps_here - 1]
    time_increment = 0
    block_map = matmul(step_ops[time_increment], block_map)
    block_vec = matmul(step_ops[time_increment], block_vec) + sources[time_increment]
    identity = (jnp.eye(width, dtype=jnp.float32), jnp.zeros((width,), jnp.float32))
    prefix = prefix_2((block_map, block_vec), "tm", combine, identity)
    lam_end = matmul(prefix[0], terminal) + prefix[1]
    states = []
    lam = lam_end
    for time_increment in range(steps_here - 1, -1, -1):
        lam = matmul(step_ops[time_increment], lam) + sources[time_increment]
        states.append(lam)
    adjoint_states = jnp.stack(states[::-1], axis=0)
    columns = lax.broadcasted_iota(jnp.int32, (gen_bus.shape[0], width), 1)
    selector = (columns == gen_bus[:, None]).astype(jnp.float32)
    picked = matmul(adjoint_states, selector.T)
    share = jnp.sum(picked * inertia_jac, axis=0)
    total = lax.psum(share, "tm")
    total_steps = steps_here * lax.axis_size("tm")
    sensitivity = total * float(total_steps) ** (-0.5)
    return (adjoint_states, sensitivity)


def solution(mesh):
    in_specs = (P("tm", None, None), P("tm", None), P(), P("tm", None), P())
    out_specs = (P("tm", None), P())
    return jax.shard_map(
        on_device, mesh=mesh, in_specs=in_specs, out_specs=out_specs, check_vma=False
    )
```

profile of v0, /device:TPU:1, one launch (start us, length us, event | category | flops | bytes accessed | tf_op | source)
XLA Modules:
  0.0 1046.5 jit_solution(16165328054481829497)
XLA Ops:
  7.2 2.1 fusion.10
  11.4 67.2 %all-gather.2 = f32[256,1,256]{2,1,0:T(1,128)S(1)} all-gather(f32[1,1,256]{2,1,0:T(1,128)S(1)} %bitcast.72), channel_id=3, replica_groups=mesh['tm'=256] {'tm'}, dimensions={0}, use_global_device_ids=true | all-gather | bytes 263168 | tf_op jit(solution)/shard_map/all_gather | solution.py:9
  78.8 149.0 %all-gather.5.cloned.1.call-done = f32[65536,256]{1,0:T(8,128)} async-done(((f32[256,256]{1,0:T(8,128)}), f32[65536,256]{1,0:T(8,128)}) %all-gather.5.cloned.1.call-update) | async-done | bytes 67108880 | tf_op jit(solution)/shard_map/all_gather | solution.py:9
  227.8 44.2 %rev.6 = f32[256,256,256]{2,1,0:T(8,128)} reverse(f32[256,256,256]{2,1,0:T(8,128)} %bitcast.2), dimensions={0} | reverse | bytes 134217728 | tf_op jit(solution)/shard_map/rev | solution.py:10
  272.0 691.4 %while.16 = (s32[]{:T(128)}, f32[256,256]{1,0:T(8,128)S(1)}, f32[256]{0:T(256)S(1)}, s32[]{:T(128)}, f32[256,256,256]{2,1,0:T(8,128)}, /*index=5*/f32[256,256]{1,0:T(8,128)S(1)}, s32[]{:T(128)}, s32[]{:T(128)}) while((s32[]{:T(128)}, f32[256,256]{1,0:T(8,128)S(1)}, f32[256]{0:T(256)S(1)}, s32[]{:T(128)}, ...), condition=%wide.region_1.2_spmd.clone, body=%wide.region_0.1_spmd.clone.sunk | while | flops 202179584 | bytes 1845375 | solution.py:20
  272.1 1.3 convolution_select_fusion.2
  293.8 1.3 convolution_select_fusion.2
  296.5 1.3 convolution_select_fusion.2
  299.2 1.3 convolution_select_fusion.2
  301.9 1.3 convolution_select_fusion.2
  304.6 1.3 convolution_select_fusion.2
  307.3 1.3 convolution_select_fusion.2
  345.3 1.3 convolution_select_fusion.2
  348.0 1.3 convolution_select_fusion.2
  350.7 1.3 convolution_select_fusion.2
  353.4 1.3 convolution_select_fusion.2
  356.1 1.3 convolution_select_fusion.2
  358.8 1.3 convolution_select_fusion.2
  396.8 1.3 convolution_select_fusion.2
  399.5 1.3 convolution_select_fusion.2
  402.2 1.3 convolution_select_fusion.2
  404.9 1.3 convolution_select_fusion.2
  407.6 1.3 convolution_select_fusion.2
  410.4 1.3 convolution_select_fusion.2
  448.3 1.3 convolution_select_fusion.2
  451.0 1.3 convolution_select_fusion.2
  453.7 1.3 convolution_select_fusion.2
  456.5 1.3 convolution_select_fusion.2
  459.2 1.3 convolution_select_fusion.2
  461.9 1.3 convolution_select_fusion.2
  499.8 1.3 convolution_select_fusion.2
  964.8 74.4 %psum.7 = f32[64]{0:T(128)S(1)} all-reduce(f32[64]{0:T(128)S(1)} %fusion.7), channel_id=1, replica_groups=mesh['tm'=256] {'tm'}, use_global_device_ids=true, to_apply=%region_3.4 | all-reduce | flops 64 | bytes 512 | tf_op jit(solution)/shard_map/psum | solution.py:52
  (1532 shorter events, 645.5 us)
Async XLA Ops:
  7.2 956.3 %copy-start = (f32[256]{0:T(256)S(1)}, f32[256]{0:T(256)}, u32[]{:S(2)}) copy-start(f32[256]{0:T(256)} %param.9) | copy-start | bytes 3076
  7.2 220.6 %all-gather.5.cloned.1.call-start = ((), (), s32[]{:S(2)}) async-start(), calls=%async_computation | async-start | bytes 67371008 | tf_op jit(solution)/shard_map/all_gather | solution.py:9
  227.8 736.0 %copy-start.1 = (f32[2,256,256]{2,1,0:T(8,128)S(1)}, f32[2,256,256]{2,1,0:T(8,128)}, u32[]{:S(2)}) copy-start(f32[2,256,256]{2,1,0:T(8,128)} %param.7) | copy-start | bytes 1572868
  227.8 736.7 %copy-start.3 = (f32[2,64]{1,0:T(2,128)S(1)}, f32[2,64]{1,0:T(2,128)}, u32[]{:S(2)}) copy-start(f32[2,64]{1,0:T(2,128)} %param.10) | copy-start | bytes 1540
  227.8 736.7 %copy-start.4 = (s32[64]{0:T(128)S(1)}, s32[64]{0:T(128)}, u32[]{:S(2)}) copy-start(s32[64]{0:T(128)} %param.11) | copy-start | bytes 772
  964.5 75.1 %copy-start.2 = (f32[2,256]{1,0:T(2,128)}, f32[2,256]{1,0:T(2,128)S(1)}, u32[]{:S(2)}) copy-start(f32[2,256]{1,0:T(2,128)S(1)} %pad_maximum_fusion) | copy-start | bytes 6148
Sparse Core Ops, SparseCore 0:
  11.6 216.1 all-gather.4
where the time goes:
time: 1060 us; the launch traced here: 1050 us
  matrix products  656 us (62%)
  waiting for transfers between devices  149 us (14%)
  blocking collectives  142 us (13%)
  local copies, waits for them, and re-layouts  65.5 us (6%)
  loops' own time  15.3 us (1%)
  between operations  14.2 us (1%)
    dot_general x516, matrix products, matmul(): jnp.dot(left, right, precision=lax.Precision.HIGHEST, preferred_element_t...  656 us
    all_gather x1, waiting for transfers between devices, prefix_2(): pieces = jax.tree.map(lambda part: lax.all_gather(part, axis), value)  149 us
    psum x1, blocking collectives, on_device(): total = lax.psum(share, 'tm')  74.4 us
    all_gather x1, blocking collectives, prefix_2(): pieces = jax.tree.map(lambda part: lax.all_gather(part, axis), value)  67.2 us
    rev x2, local copies, waits for them, and re-layouts, prefix_2(): pieces = jax.tree.map(lambda part: part[::-1], pieces)  44.4 us
  transfers between devices with their start and end apart: 1, of which 1 were waited for; matrix products, arithmetic and copies ran while one was open for 0% of the time, Pallas kernels for 0%

commit v1 on v0

v1 whole, which is shorter than its diff:
```python
import functools

import jax
import jax.numpy as jnp
from jax import lax
from jax.experimental import pallas as pl
from jax.experimental.pallas import tpu as pltpu
from jax.sharding import PartitionSpec as P


NY, NZ, NX, NC = 4, 8, 4, 2
N = 256
G = 64
MS = N + G
V = MS
C = MS + 8
ROWS = MS + 16
HALF = ROWS // 2
W_ROWS = 2 * N + 16
F32 = jnp.float32
VM = pl.BlockSpec(memory_space=pltpu.VMEM)


def place(index):
    core = lax.rem(index, NC)
    x = lax.rem(lax.div(index, NC), NX)
    z = lax.rem(lax.div(index, NC * NX), NZ)
    y = lax.div(index, NC * NX * NZ)
    return y, z, x, core


def pairs(move):
    out = []
    for index in range(NY * NZ * NX * NC):
        y, z, x, c = index // 64, (index // 8) % 8, (index // 2) % 4, index % 2
        y, z, x, c = move(y, z, x, c)
        out.append((index, (((y % NY) * NZ + z % NZ) * NX + x % NX) * NC + c))
    return out


OTHER_CORE = pairs(lambda y, z, x, c: (y, z, x, 1 - c))
X_FROM = [pairs(lambda y, z, x, c, d=d: (y, z, x - d, c)) for d in (1, 2, 3)]
Y_FROM = [pairs(lambda y, z, x, c, d=d: (y - d, z, x, c)) for d in (1, 2, 3)]
Z_ONE = [pairs(lambda y, z, x, c: (y, z ^ 1, x, c))]
Z_FROM = [
    pairs(lambda y, z, x, c: (y, z - 2, x, c)),
    pairs(lambda y, z, x, c: (y, z ^ 5, x, c)),
    pairs(lambda y, z, x, c: (y, z + 2, x, c)),
]


def split(value):
    high = value.astype(jnp.bfloat16)
    low = (value - high.astype(F32)).astype(jnp.bfloat16)
    return high, low


def product(left, right):
    lh, ll = split(left)
    rh, rl = split(right)
    a = jnp.concatenate([lh, lh, ll], axis=1)
    b = jnp.concatenate([rh, rl, rh], axis=0)
    return jnp.dot(a, b, preferred_element_type=F32)


def times_row(matrix, row):
    p = matrix * row
    p = p[:, :128] + p[:, 128:]
    return jnp.sum(p.T, axis=0, keepdims=True)


def compose(early, late):
    (me, se, ve, ce), (ml, sl, vl, cl) = early, late
    p = product(jnp.concatenate([me, se], axis=0), ml)
    return (
        p[:N],
        p[N:] + sl,
        times_row(me, vl) + ve,
        times_row(se, vl) + ce + cl,
    )


def load(ref):
    return ref[0:N, :], ref[N:MS, :], ref[V : V + 1, :], ref[C : C + 1, 0:G]


def store(ref, value):
    m, s, v, c = value
    ref[0:N, :] = m
    ref[N:MS, :] = s
    ref[V : V + 8, :] = jnp.broadcast_to(v, (8, N))
    ref[C : C + 8, :] = jnp.zeros((8, N), F32)
    ref[C : C + 1, 0:G] = c


def store_half(half_ref, ref, core):
    half_ref[...] = ref[pl.ds(pl.multiple_of(core * HALF, 8), HALF), :]


def me():
    return place(lax.axis_index("tm"))


def leaf_kernel(a_ref, row_ref, t_ref):
    a0, a1 = a_ref[0], a_ref[1]
    s0, s1 = row_ref[0:1, :], row_ref[1:2, :]
    m = product(a0, a1)
    v = times_row(a0, s1) + s0
    eye = (
        lax.broadcasted_iota(jnp.int32, (G, G), 0)
        == lax.broadcasted_iota(jnp.int32, (G, G), 1)
    ).astype(F32)
    column = lambda row: jnp.sum(eye * row, axis=1, keepdims=True)
    as_row = lambda col: jnp.sum(eye * col, axis=0, keepdims=True)
    states = lax.broadcasted_iota(jnp.int32, (G, N), 1).astype(F32)
    chosen = jnp.where(states == column(row_ref[4:5, 0:G]), 1.0, 0.0)
    d0 = chosen * column(row_ref[2:3, 0:G])
    d1 = chosen * column(row_ref[3:4, 0:G])
    s = product(d0, m) + product(d1, a1)
    c = as_row(jnp.sum(d0 * v + d1 * s1, axis=1, keepdims=True))
    store(t_ref, (m, s, v, c))


def pick(first, a, b):
    return (
        tuple(jnp.where(first, p, q) for p, q in zip(a, b)),
        tuple(jnp.where(first, q, p) for p, q in zip(a, b)),
    )


def core_kernel(mine_ref, other_ref, t_ref, half_ref):
    core = me()[3]
    early, late = pick(core == 0, load(mine_ref), load(other_ref))
    store(t_ref, compose(early, late))
    store_half(half_ref, t_ref, core)


def pair_kernel(mine_ref, direct_ref, swapped_ref, t_ref, half_ref, other_ref):
    _, z, _, core = me()
    other_ref[pl.ds(pl.multiple_of(core * HALF, 8), HALF), :] = direct_ref[...]
    other_ref[pl.ds(pl.multiple_of((1 - core) * HALF, 8), HALF), :] = swapped_ref[...]
    first = lax.rem(z, 2) == 0
    early, late = pick(first, load(mine_ref), load(other_ref))
    store(t_ref, compose(early, late))
    store_half(half_ref, t_ref, core)


def fill(slots_ref, at, core, mine_ref, direct, swapped):
    slots_ref[at] = mine_ref[...]
    for d in (1, 2, 3):
        slot = lax.rem(at + d, 4)
        slots_ref[slot, pl.ds(pl.multiple_of(core * HALF, 8), HALF), :] = direct[d - 1][...]
        slots_ref[slot, pl.ds(pl.multiple_of((1 - core) * HALF, 8), HALF), :] = swapped[d - 1][...]


def quad_at(axis, z, x):
    return x if axis == "x" else lax.div(z, 2)


def quad_kernel(axis, mine_ref, d1, d2, d3, s1, s2, s3, t_ref, half_ref, slots_ref, tb_ref):
    _, z, x, core = me()
    fill(slots_ref, quad_at(axis, z, x), core, mine_ref, (d1, d2, d3), (s1, s2, s3))
    tb = compose(load(slots_ref.at[2]), load(slots_ref.at[3]))
    ta = compose(load(slots_ref.at[0]), load(slots_ref.at[1]))
    store(tb_ref, tb)
    store(t_ref, compose(ta, tb))
    store_half(half_ref, t_ref, core)


def extend(w_ref, late_m, late_v, out_ref):
    out_ref[0 : 2 * N, :] = product(w_ref[0 : 2 * N, :], late_m)
    for state in (0, 1):
        at = 2 * N + 8 * state
        offset = times_row(w_ref[N * state : N * (state + 1), :], late_v)
        out_ref[at : at + 8, :] = w_ref[at : at + 8, :] + offset


def own_core_kernel(t_ref, a_ref, row_ref, other_ref, out_ref, w_ref):
    w_ref[0:N, :] = t_ref[0:N, :]
    w_ref[N : 2 * N, :] = a_ref[1]
    w_ref[2 * N : 2 * N + 8, :] = t_ref[V : V + 8, :]
    w_ref[2 * N + 8 :, :] = jnp.broadcast_to(row_ref[1:2, :], (8, N))
    own_pair(me()[3], w_ref, other_ref, out_ref)


def own_pair_kernel(w_ref, late_ref, out_ref):
    own_pair(lax.rem(me()[1], 2), w_ref, late_ref, out_ref)


def own_pair(bit, w_ref, late_ref, out_ref):
    @pl.when(bit == 0)
    def _():
        extend(w_ref, late_ref[0:N, :], late_ref[V : V + 1, :], out_ref)

    @pl.when(bit != 0)
    def _():
        out_ref[...] = w_ref[...]


def own_quad_kernel(axis, w_ref, slots_ref, tb_ref, out_ref):
    _, z, x, _ = me()
    at = quad_at(axis, z, x)

    @pl.when(at == 0)
    def _():
        m1, v1 = slots_ref[1, 0:N, :], slots_ref[1, V : V + 1, :]
        late_m = product(m1, tb_ref[0:N, :])
        late_v = times_row(m1, tb_ref[V : V + 1, :]) + v1
        extend(w_ref, late_m, late_v, out_ref)

    @pl.when(at == 1)
    def _():
        extend(w_ref, tb_ref[0:N, :], tb_ref[V : V + 1, :], out_ref)

    @pl.when(at == 2)
    def _():
        extend(w_ref, slots_ref[3, 0:N, :], slots_ref[3, V : V + 1, :], out_ref)

    @pl.when(at == 3)
    def _():
        out_ref[...] = w_ref[...]


def last_kernel(scale, mine_ref, d1, d2, d3, s1, s2, s3, w_ref, end_ref, states_ref, sens_ref, slots_ref):
    y, _, _, core = me()
    fill(slots_ref, y, core, mine_ref, (d1, d2, d3), (s1, s2, s3))
    lam = end_ref[...]
    here = lam
    total = jnp.zeros((1, G), F32)
    for q in (3, 2, 1, 0):
        here = jnp.where(y == q, lam, here)
        m, s, v, c = load(slots_ref.at[q])
        total = total + times_row(s, lam) + c
        lam = times_row(m, lam) + v
    sens_ref[...] = total * scale
    for state in (0, 1):
        at = 2 * N + 8 * state
        states_ref[state : state + 1, :] = (
            times_row(w_ref[N * state : N * (state + 1), :], here) + w_ref[at : at + 1, :]
        )


def call(kernel, outs, args, scratch=(), products=1):
    shapes = [jax.ShapeDtypeStruct(o, F32) for o in outs]
    return pl.pallas_call(
        kernel,
        out_shape=shapes,
        in_specs=[VM] * len(args),
        out_specs=[VM] * len(outs),
        scratch_shapes=list(scratch),
        compiler_params=pltpu.CompilerParams(vmem_limit_bytes=16 << 20),
        cost_estimate=pl.CostEstimate(
            flops=products * 6 * MS * N * N, bytes_accessed=1 << 20, transcendentals=0
        ),
    )(*args)


def exchange(half, moves):
    direct, swapped = [], []
    for move in moves:
        direct.append(lax.ppermute(half, "tm", move))
    for part in direct:
        swapped.append(lax.ppermute(part, "tm", OTHER_CORE))
    return direct, swapped


def local(step_ops, sources, terminal, inertia_jac, gen_bus):
    t, h, w = (ROWS, N), (HALF, N), (W_ROWS, N)
    part = functools.partial
    wide = lambda rows: jnp.pad(rows, ((0, 0), (0, N - G)))
    rows = jnp.concatenate(
        [sources, wide(inertia_jac), wide(gen_bus.astype(F32).reshape(1, G)), jnp.zeros((3, N), F32)]
    )
    (leaf,) = call(leaf_kernel, [t], [step_ops, rows])
    total = leaf
    other = lax.ppermute(total, "tm", OTHER_CORE)
    total, half = call(core_kernel, [t, h], [total, other])

    direct, swapped = exchange(half, X_FROM)
    (own,) = call(own_core_kernel, [w], [leaf, step_ops, rows, other], scratch=[pltpu.VMEM(w, F32)])
    total, half, slots, tb = call(
        part(quad_kernel, "x"), [t, h, (4,) + t, t], [total, *direct, *swapped], products=3
    )

    direct, swapped = exchange(half, Z_ONE)
    (own,) = call(part(own_quad_kernel, "x"), [w], [own, slots, tb], products=2)
    total, half, late = call(pair_kernel, [t, h, t], [total, *direct, *swapped])

    direct, swapped = exchange(half, Z_FROM)
    (own,) = call(own_pair_kernel, [w], [own, late])
    total, half, slots, tb = call(
        part(quad_kernel, "z"), [t, h, (4,) + t, t], [total, *direct, *swapped], products=3
    )

    direct, swapped = exchange(half, Y_FROM)
    (own,) = call(part(own_quad_kernel, "z"), [w], [own, slots, tb], products=2)
    steps = step_ops.shape[0] * lax.axis_size("tm")
    states, sens = call(
        part(last_kernel, float(steps) ** -0.5),
        [(2, N), (1, G)],
        [total, *direct, *swapped, own, terminal.reshape(1, N)],
        scratch=[pltpu.VMEM((4,) + t, F32)],
    )
    return states, sens.reshape(G)


def solution(mesh):
    in_specs = (P("tm", None, None), P("tm", None), P(), P("tm", None), P())
    out_specs = (P("tm", None), P())
    return jax.shard_map(local, mesh=mesh, in_specs=in_specs, out_specs=out_specs, check_vma=False)
```

time: 1060 us -> 73.6 us (0.07); the launches traced: 1050 us -> 73.5 us
  matrix products: 656 us -> 0 us
  blocking collectives: 142 us -> 0 us
  waiting for transfers between devices: 149 us -> 29.2 us
  local copies, waits for them, and re-layouts: 65.5 us -> 1.13 us
  starting transfers between devices: 0.04 us -> 34.1 us
  loops' own time: 15.3 us -> 0 us
  between operations: 14.2 us -> 0.77 us
    dot_general x516 -> x0, matrix products: 656 us -> none  [matmul(): jnp.dot(left, right, precision=lax.Precision.HIGHEST, preferred_element_t...]
    all_gather x1 -> x0, waiting for transfers between devices: 149 us -> none  [prefix_2(): pieces = jax.tree.map(lambda part: lax.all_gather(part, axis), value)]
    psum x1 -> x0, blocking collectives: 74.4 us -> none  [on_device(): total = lax.psum(share, 'tm')]
    all_gather x1 -> x0, blocking collectives: 67.2 us -> none  [prefix_2(): pieces = jax.tree.map(lambda part: lax.all_gather(part, axis), value)]
    rev x2 -> x0, local copies, waits for them, and re-layouts: 44.4 us -> none  [prefix_2(): pieces = jax.tree.map(lambda part: part[::-1], pieces)]
    ppermute x0 -> x21, starting transfers between devices: none -> 34.1 us  [the longest x10 18.3 us: exchange(): direct.append(lax.ppermute(half, 'tm', move))]
    ppermute x0 -> x21, waiting for transfers between devices: none -> 29.2 us  [the longest x10 24.8 us: exchange(): direct.append(lax.ppermute(half, 'tm', move))]
    dynamic_slice x255 -> x0, local copies, waits for them, and re-layouts: 15.4 us -> none  [turn(): longer = join(running, jax.tree.map(lambda part: part[position], pieces))]
  transfers between devices with their start and end apart: 1 -> 21, of which waited for: 1 -> 13; matrix products, arithmetic and copies ran while one was open for 0% -> 0% of each run, Pallas kernels for 0% -> 3%
where the time goes in v1:
time: 73.6 us; the launch traced here: 73.5 us
  starting transfers between devices  34.1 us (46%)
  waiting for transfers between devices  29.2 us (40%)
  Pallas kernels  6.78 us (9%)
  other arithmetic  1.43 us (2%)
  local copies, waits for them, and re-layouts  1.13 us (2%)
  between operations  0.77 us (1%)
    ppermute x10, waiting for transfers between devices, exchange(): direct.append(lax.ppermute(half, 'tm', move))  24.8 us
    ppermute x10, starting transfers between devices, exchange(): direct.append(lax.ppermute(half, 'tm', move))  18.3 us
    ppermute x10, starting transfers between devices, exchange(): swapped.append(lax.ppermute(part, 'tm', OTHER_CORE))  12.5 us
    pallas_call x10, Pallas kernels, call(): pl.pallas_call(kernel, out_shape=shapes, in_specs=[VM] * len(args), out_s...  6.78 us
    ppermute x1, starting transfers between devices, local(): other = lax.ppermute(total, 'tm', OTHER_CORE)  3.29 us
    ppermute x10, waiting for transfers between devices, exchange(): swapped.append(lax.ppermute(part, 'tm', OTHER_CORE))  3.12 us
  transfers between devices with their start and end apart: 21, of which 13 were waited for; matrix products, arithmetic and copies ran while one was open for 0% of the time, Pallas kernels for 3%

profile of v1, /device:TPU:1, one launch (start us, length us, event | category | flops | bytes accessed | tf_op | source)
XLA Modules:
  0.0 73.5 jit_solution(5670580063953067714)
XLA Ops:
  2.1 1.0 %copy-done = f32[2,256,256]{2,1,0:T(8,128)S(1)} copy-done((f32[2,256,256]{2,1,0:T(8,128)S(1)}, f32[2,256,256]{2,1,0:T(8,128)}, u32[]{:S(2)}) %copy-start) | copy-done | bytes 524312
  3.7 3.3 %collective-permute-start = (f32[336,256]{1,0:T(8,128)S(1)}, f32[336,256]{1,0:T(8,128)S(1)}, u32[]{:S(2)}, u32[]{:S(2)}) collective-permute-start(f32[336,256]{1,0:T(8,128)S(1)} %shard_map.68.mine_ref.t_ref), channel_id=1, source_target_pairs={{0,1},{1,0},{2,3},{3,2},{4,5},{5,4},{6,7},{7,6},{8,9},{9,8},{10,11... | collective-permute-start | bytes 1032200 | tf_op jit(solution)/shard_map/ppermute | solution.py:276
  7.0 1.3 %collective-permute-done.other_ref = f32[336,256]{1,0:T(8,128)S(1)} collective-permute-done((f32[336,256]{1,0:T(8,128)S(1)}, f32[336,256]{1,0:T(8,128)S(1)}, u32[]{:S(2)}, u32[]{:S(2)}) %collective-permute-start) | collective-permute-done | bytes 344096 | tf_op jit(solution)/shard_map/ppermute | solution.py:276
  8.8 1.9 %collective-permute-start.2 = (f32[168,256]{1,0:T(8,128)S(1)}, f32[168,256]{1,0:T(8,128)S(1)}, u32[]{:S(2)}, u32[]{:S(2)}) collective-permute-start(f32[168,256]{1,0:T(8,128)S(1)} %get-tuple-element.18), channel_id=1, source_target_pairs={{0,4},{1,5},{2,6},{3,7},{4,0},{5,1},{6,2},{7,3},{8,12},{9,13},{10,... | collective-permute-start | bytes 516104 | tf_op jit(solution)/shard_map/ppermute | solution.py:261
  10.7 1.2 %collective-permute-start.1 = (f32[168,256]{1,0:T(8,128)S(1)}, f32[168,256]{1,0:T(8,128)S(1)}, u32[]{:S(2)}, u32[]{:S(2)}) collective-permute-start(f32[168,256]{1,0:T(8,128)S(1)} %get-tuple-element.18), channel_id=1, source_target_pairs={{0,6},{1,7},{2,0},{3,1},{4,2},{5,3},{6,4},{7,5},{8,14},{9,15},{10,... | collective-permute-start | bytes 516104 | tf_op jit(solution)/shard_map/ppermute | solution.py:261
  11.9 4.4 %collective-permute-done.3.d3 = f32[168,256]{1,0:T(8,128)S(1)} collective-permute-done((f32[168,256]{1,0:T(8,128)S(1)}, f32[168,256]{1,0:T(8,128)S(1)}, u32[]{:S(2)}, u32[]{:S(2)}) %collective-permute-start.3) | collective-permute-done | bytes 172064 | tf_op jit(solution)/shard_map/ppermute | solution.py:261
  16.3 4.2 %collective-permute-start.6 = (f32[168,256]{1,0:T(8,128)S(1)}, f32[168,256]{1,0:T(8,128)S(1)}, u32[]{:S(2)}, u32[]{:S(2)}) collective-permute-start(f32[168,256]{1,0:T(8,128)S(1)} %collective-permute-done.3.d3), channel_id=1, source_target_pairs={{0,1},{1,0},{2,3},{3,2},{4,5},{5,4},{6,7},{7,6},{8,9},{9,8},{10,11... | collective-permute-start | bytes 516104 | tf_op jit(solution)/shard_map/ppermute | solution.py:263
  22.1 1.0 %shard_map.70 = (f32[336,256]{1,0:T(8,128)S(1)}, f32[168,256]{1,0:T(8,128)S(1)}, f32[4,336,256]{2,1,0:T(8,128)S(1)}, f32[336,256]{1,0:T(8,128)S(1)}) custom-call(f32[336,256]{1,0:T(8,128)S(1)} %get-tuple-element.17.mine_ref, f32[168,256]{1,0:T(8,128)S(1)} %collective-permute-done.1.d1, f32[168,256]{1,0:T(8,128)S(1)} %collective-permute-done.2.d2, ...), custom_call_target="tpu_custom_call" | custom-call | flops 377487360 | bytes 1048576 | tf_op jit(solution)/shard_map/pallas_call | solution.py:245
  23.9 4.9 %collective-permute-done.7.direct_ref = f32[168,256]{1,0:T(8,128)S(1)} collective-permute-done((f32[168,256]{1,0:T(8,128)S(1)}, f32[168,256]{1,0:T(8,128)S(1)}, u32[]{:S(2)}, u32[]{:S(2)}) %collective-permute-start.7) | collective-permute-done | bytes 172064 | tf_op jit(solution)/shard_map/ppermute | solution.py:261
  28.8 1.2 %collective-permute-start.8 = (f32[168,256]{1,0:T(8,128)S(1)}, f32[168,256]{1,0:T(8,128)S(1)}, u32[]{:S(2)}, u32[]{:S(2)}) collective-permute-start(f32[168,256]{1,0:T(8,128)S(1)} %collective-permute-done.7.direct_ref), channel_id=1, source_target_pairs={{0,1},{1,0},{2,3},{3,2},{4,5},{5,4},{6,7},{7,6},{8,9},{9,8},{10,11... | collective-permute-start | bytes 516104 | tf_op jit(solution)/shard_map/ppermute | solution.py:263
  30.0 1.0 %collective-permute-done.8.swapped_ref = f32[168,256]{1,0:T(8,128)S(1)} collective-permute-done((f32[168,256]{1,0:T(8,128)S(1)}, f32[168,256]{1,0:T(8,128)S(1)}, u32[]{:S(2)}, u32[]{:S(2)}) %collective-permute-start.8) | collective-permute-done | bytes 172064 | tf_op jit(solution)/shard_map/ppermute | solution.py:263
  31.5 2.3 %collective-permute-start.11 = (f32[168,256]{1,0:T(8,128)S(1)}, f32[168,256]{1,0:T(8,128)S(1)}, u32[]{:S(2)}, u32[]{:S(2)}) collective-permute-start(f32[168,256]{1,0:T(8,128)S(1)} %get-tuple-element.22), channel_id=1, source_target_pairs={{0,16},{1,17},{2,18},{3,19},{4,20},{5,21},{6,22},{7,23},{8,24},{9,... | collective-permute-start | bytes 516104 | tf_op jit(solution)/shard_map/ppermute | solution.py:261
  33.7 4.5 %collective-permute-start.10 = (f32[168,256]{1,0:T(8,128)S(1)}, f32[168,256]{1,0:T(8,128)S(1)}, u32[]{:S(2)}, u32[]{:S(2)}) collective-permute-start(f32[168,256]{1,0:T(8,128)S(1)} %get-tuple-element.22), channel_id=1, source_target_pairs={{0,40},{1,41},{2,42},{3,43},{4,44},{5,45},{6,46},{7,47},{8,32},{9,... | collective-permute-start | bytes 516104 | tf_op jit(solution)/shard_map/ppermute | solution.py:261
  38.2 2.4 %collective-permute-start.9 = (f32[168,256]{1,0:T(8,128)S(1)}, f32[168,256]{1,0:T(8,128)S(1)}, u32[]{:S(2)}, u32[]{:S(2)}) collective-permute-start(f32[168,256]{1,0:T(8,128)S(1)} %get-tuple-element.22), channel_id=1, source_target_pairs={{0,48},{1,49},{2,50},{3,51},{4,52},{5,53},{6,54},{7,55},{8,56},{9,... | collective-permute-start | bytes 516104 | tf_op jit(solution)/shard_map/ppermute | solution.py:261
  40.6 1.0 %collective-permute-done.11.d3 = f32[168,256]{1,0:T(8,128)S(1)} collective-permute-done((f32[168,256]{1,0:T(8,128)S(1)}, f32[168,256]{1,0:T(8,128)S(1)}, u32[]{:S(2)}, u32[]{:S(2)}) %collective-permute-start.11) | collective-permute-done | bytes 172064 | tf_op jit(solution)/shard_map/ppermute | solution.py:261
  41.6 1.9 %collective-permute-start.14 = (f32[168,256]{1,0:T(8,128)S(1)}, f32[168,256]{1,0:T(8,128)S(1)}, u32[]{:S(2)}, u32[]{:S(2)}) collective-permute-start(f32[168,256]{1,0:T(8,128)S(1)} %collective-permute-done.11.d3), channel_id=1, source_target_pairs={{0,1},{1,0},{2,3},{3,2},{4,5},{5,4},{6,7},{7,6},{8,9},{9,8},{10,11... | collective-permute-start | bytes 516104 | tf_op jit(solution)/shard_map/ppermute | solution.py:263
  43.5 7.0 %collective-permute-done.10.d2 = f32[168,256]{1,0:T(8,128)S(1)} collective-permute-done((f32[168,256]{1,0:T(8,128)S(1)}, f32[168,256]{1,0:T(8,128)S(1)}, u32[]{:S(2)}, u32[]{:S(2)}) %collective-permute-start.10) | collective-permute-done | bytes 172064 | tf_op jit(solution)/shard_map/ppermute | solution.py:261
  50.5 1.1 %collective-permute-start.13 = (f32[168,256]{1,0:T(8,128)S(1)}, f32[168,256]{1,0:T(8,128)S(1)}, u32[]{:S(2)}, u32[]{:S(2)}) collective-permute-start(f32[168,256]{1,0:T(8,128)S(1)} %collective-permute-done.10.d2), channel_id=1, source_target_pairs={{0,1},{1,0},{2,3},{3,2},{4,5},{5,4},{6,7},{7,6},{8,9},{9,8},{10,11... | collective-permute-start | bytes 516104 | tf_op jit(solution)/shard_map/ppermute | solution.py:263
  51.5 2.0 %collective-permute-done.9.d1 = f32[168,256]{1,0:T(8,128)S(1)} collective-permute-done((f32[168,256]{1,0:T(8,128)S(1)}, f32[168,256]{1,0:T(8,128)S(1)}, u32[]{:S(2)}, u32[]{:S(2)}) %collective-permute-start.9) | collective-permute-done | bytes 172064 | tf_op jit(solution)/shard_map/ppermute | solution.py:261
  53.5 1.2 %collective-permute-start.12 = (f32[168,256]{1,0:T(8,128)S(1)}, f32[168,256]{1,0:T(8,128)S(1)}, u32[]{:S(2)}, u32[]{:S(2)}) collective-permute-start(f32[168,256]{1,0:T(8,128)S(1)} %collective-permute-done.9.d1), channel_id=1, source_target_pairs={{0,1},{1,0},{2,3},{3,2},{4,5},{5,4},{6,7},{7,6},{8,9},{9,8},{10,11... | collective-permute-start | bytes 516104 | tf_op jit(solution)/shard_map/ppermute | solution.py:263
  54.7 1.0 %collective-permute-done.12.s1 = f32[168,256]{1,0:T(8,128)S(1)} collective-permute-done((f32[168,256]{1,0:T(8,128)S(1)}, f32[168,256]{1,0:T(8,128)S(1)}, u32[]{:S(2)}, u32[]{:S(2)}) %collective-permute-start.12) | collective-permute-done | bytes 172064 | tf_op jit(solution)/shard_map/ppermute | solution.py:263
  55.7 1.0 %shard_map.72 = (f32[336,256]{1,0:T(8,128)S(1)}, f32[168,256]{1,0:T(8,128)S(1)}, f32[4,336,256]{2,1,0:T(8,128)S(1)}, f32[336,256]{1,0:T(8,128)S(1)}) custom-call(f32[336,256]{1,0:T(8,128)S(1)} %get-tuple-element.21.mine_ref, f32[168,256]{1,0:T(8,128)S(1)} %collective-permute-done.9.d1, f32[168,256]{1,0:T(8,128)S(1)} %collective-permute-done.10.d2, ...), custom_call_target="tpu_custom_call" | custom-call | flops 377487360 | bytes 1048576 | tf_op jit(solution)/shard_map/pallas_call | solution.py:245
  56.8 1.6 %collective-permute-start.17 = (f32[168,256]{1,0:T(8,128)S(1)}, f32[168,256]{1,0:T(8,128)S(1)}, u32[]{:S(2)}, u32[]{:S(2)}) collective-permute-start(f32[168,256]{1,0:T(8,128)S(1)} %get-tuple-element.24), channel_id=1, source_target_pairs={{0,64},{1,65},{2,66},{3,67},{4,68},{5,69},{6,70},{7,71},{8,72},{9,... | collective-permute-start | bytes 516104 | tf_op jit(solution)/shard_map/ppermute | solution.py:261
  58.3 2.6 %collective-permute-start.16 = (f32[168,256]{1,0:T(8,128)S(1)}, f32[168,256]{1,0:T(8,128)S(1)}, u32[]{:S(2)}, u32[]{:S(2)}) collective-permute-start(f32[168,256]{1,0:T(8,128)S(1)} %get-tuple-element.24), channel_id=1, source_target_pairs={{0,128},{1,129},{2,130},{3,131},{4,132},{5,133},{6,134},{7,135},{8... | collective-permute-start | bytes 516104 | tf_op jit(solution)/shard_map/ppermute | solution.py:261
  60.9 1.1 %collective-permute-start.15 = (f32[168,256]{1,0:T(8,128)S(1)}, f32[168,256]{1,0:T(8,128)S(1)}, u32[]{:S(2)}, u32[]{:S(2)}) collective-permute-start(f32[168,256]{1,0:T(8,128)S(1)} %get-tuple-element.24), channel_id=1, source_target_pairs={{0,192},{1,193},{2,194},{3,195},{4,196},{5,197},{6,198},{7,199},{8... | collective-permute-start | bytes 516104 | tf_op jit(solution)/shard_map/ppermute | solution.py:261
  62.0 1.9 %collective-permute-done.17.d3 = f32[168,256]{1,0:T(8,128)S(1)} collective-permute-done((f32[168,256]{1,0:T(8,128)S(1)}, f32[168,256]{1,0:T(8,128)S(1)}, u32[]{:S(2)}, u32[]{:S(2)}) %collective-permute-start.17) | collective-permute-done | bytes 172064 | tf_op jit(solution)/shard_map/ppermute | solution.py:261
  63.9 1.1 %collective-permute-start.20 = (f32[168,256]{1,0:T(8,128)S(1)}, f32[168,256]{1,0:T(8,128)S(1)}, u32[]{:S(2)}, u32[]{:S(2)}) collective-permute-start(f32[168,256]{1,0:T(8,128)S(1)} %collective-permute-done.17.d3), channel_id=1, source_target_pairs={{0,1},{1,0},{2,3},{3,2},{4,5},{5,4},{6,7},{7,6},{8,9},{9,8},{10,11... | collective-permute-start | bytes 516104 | tf_op jit(solution)/shard_map/ppermute | solution.py:263
  65.1 3.7 %collective-permute-done.16.d2 = f32[168,256]{1,0:T(8,128)S(1)} collective-permute-done((f32[168,256]{1,0:T(8,128)S(1)}, f32[168,256]{1,0:T(8,128)S(1)}, u32[]{:S(2)}, u32[]{:S(2)}) %collective-permute-start.16) | collective-permute-done | bytes 172064 | tf_op jit(solution)/shard_map/ppermute | solution.py:261
  68.7 1.2 %collective-permute-start.19 = (f32[168,256]{1,0:T(8,128)S(1)}, f32[168,256]{1,0:T(8,128)S(1)}, u32[]{:S(2)}, u32[]{:S(2)}) collective-permute-start(f32[168,256]{1,0:T(8,128)S(1)} %collective-permute-done.16.d2), channel_id=1, source_target_pairs={{0,1},{1,0},{2,3},{3,2},{4,5},{5,4},{6,7},{7,6},{8,9},{9,8},{10,11... | collective-permute-start | bytes 516104 | tf_op jit(solution)/shard_map/ppermute | solution.py:263
  70.0 0.8 %shard_map.74.w_ref = f32[528,256]{1,0:T(8,128)S(1)} custom-call(f32[528,256]{1,0:T(8,128)S(1)} %shard_map.73.w_ref, f32[4,336,256]{2,1,0:T(8,128)S(1)} %get-tuple-element.25.slots_ref, f32[336,256]{1,0:T(8,128)S(1)} %get-tuple-element.26.tb_ref), custom_call_target="tpu_custom_call" | custom-call | flops 251658240 | bytes 1048576 | tf_op jit(solution)/shard_map/pallas_call | solution.py:245
  71.3 0.8 %shard_map.76.w_ref = f32[528,256]{1,0:T(8,128)S(1)} custom-call(f32[528,256]{1,0:T(8,128)S(1)} %shard_map.75.w_ref, f32[4,336,256]{2,1,0:T(8,128)S(1)} %get-tuple-element.28.slots_ref, f32[336,256]{1,0:T(8,128)S(1)} %get-tuple-element.29.tb_ref), custom_call_target="tpu_custom_call" | custom-call | flops 251658240 | bytes 1048576 | tf_op jit(solution)/shard_map/pallas_call | solution.py:245
  72.2 1.3 %shard_map.77 = (f32[2,256]{1,0:T(2,128)}, f32[1,64]{1,0:T(1,128)}) custom-call(f32[336,256]{1,0:T(8,128)S(1)} %get-tuple-element.23.mine_ref, f32[168,256]{1,0:T(8,128)S(1)} %collective-permute-done.15.d1, f32[168,256]{1,0:T(8,128)S(1)} %collective-permute-done.16.d2, f32[168,256]{1,0:T(8,128)S(1)} %collective-permute-done.17.d3, ...), custom_call_target="tpu_custom_call" | custom-call | flops 125829120 | bytes 1048576 | tf_op jit(solution)/shard_map/pallas_call | solution.py:245
  (30 shorter events, 5.9 us)
Async XLA Ops:
  2.1 1.0 %copy-start = (f32[2,256,256]{2,1,0:T(8,128)S(1)}, f32[2,256,256]{2,1,0:T(8,128)}, u32[]{:S(2)}) copy-start(f32[2,256,256]{2,1,0:T(8,128)} %a_ref.3) | copy-start | bytes 1572868
  3.7 4.6 %collective-permute-start = (f32[336,256]{1,0:T(8,128)S(1)}, f32[336,256]{1,0:T(8,128)S(1)}, u32[]{:S(2)}, u32[]{:S(2)}) collective-permute-start(f32[336,256]{1,0:T(8,128)S(1)} %shard_map.68.mine_ref.t_ref), channel_id=1, source_target_pairs={{0,1},{1,0},{2,3},{3,2},{4,5},{5,4},{6,7},{7,6},{8,9},{9,8},{10,11... | collective-permute-start | bytes 1032200 | tf_op jit(solution)/shard_map/ppermute | solution.py:276
  8.7 7.6 %collective-permute-start.3 = (f32[168,256]{1,0:T(8,128)S(1)}, f32[168,256]{1,0:T(8,128)S(1)}, u32[]{:S(2)}, u32[]{:S(2)}) collective-permute-start(f32[168,256]{1,0:T(8,128)S(1)} %get-tuple-element.18), channel_id=1, source_target_pairs={{0,2},{1,3},{2,4},{3,5},{4,6},{5,7},{6,0},{7,1},{8,10},{9,11},{10,... | collective-permute-start | bytes 516104 | tf_op jit(solution)/shard_map/ppermute | solution.py:261
  8.8 11.7 %collective-permute-start.2 = (f32[168,256]{1,0:T(8,128)S(1)}, f32[168,256]{1,0:T(8,128)S(1)}, u32[]{:S(2)}, u32[]{:S(2)}) collective-permute-start(f32[168,256]{1,0:T(8,128)S(1)} %get-tuple-element.18), channel_id=1, source_target_pairs={{0,4},{1,5},{2,6},{3,7},{4,0},{5,1},{6,2},{7,3},{8,12},{9,13},{10,... | collective-permute-start | bytes 516104 | tf_op jit(solution)/shard_map/ppermute | solution.py:261
  10.7 9.7 %collective-permute-start.1 = (f32[168,256]{1,0:T(8,128)S(1)}, f32[168,256]{1,0:T(8,128)S(1)}, u32[]{:S(2)}, u32[]{:S(2)}) collective-permute-start(f32[168,256]{1,0:T(8,128)S(1)} %get-tuple-element.18), channel_id=1, source_target_pairs={{0,6},{1,7},{2,0},{3,1},{4,2},{5,3},{6,4},{7,5},{8,14},{9,15},{10,... | collective-permute-start | bytes 516104 | tf_op jit(solution)/shard_map/ppermute | solution.py:261
  16.3 5.2 %collective-permute-start.6 = (f32[168,256]{1,0:T(8,128)S(1)}, f32[168,256]{1,0:T(8,128)S(1)}, u32[]{:S(2)}, u32[]{:S(2)}) collective-permute-start(f32[168,256]{1,0:T(8,128)S(1)} %collective-permute-done.3.d3), channel_id=1, source_target_pairs={{0,1},{1,0},{2,3},{3,2},{4,5},{5,4},{6,7},{7,6},{8,9},{9,8},{10,11... | collective-permute-start | bytes 516104 | tf_op jit(solution)/shard_map/ppermute | solution.py:263
  20.5 1.4 %collective-permute-start.5 = (f32[168,256]{1,0:T(8,128)S(1)}, f32[168,256]{1,0:T(8,128)S(1)}, u32[]{:S(2)}, u32[]{:S(2)}) collective-permute-start(f32[168,256]{1,0:T(8,128)S(1)} %collective-permute-done.2.d2), channel_id=1, source_target_pairs={{0,1},{1,0},{2,3},{3,2},{4,5},{5,4},{6,7},{7,6},{8,9},{9,8},{10,11... | collective-permute-start | bytes 516104 | tf_op jit(solution)/shard_map/ppermute | solution.py:263
  20.5 1.6 %collective-permute-start.4 = (f32[168,256]{1,0:T(8,128)S(1)}, f32[168,256]{1,0:T(8,128)S(1)}, u32[]{:S(2)}, u32[]{:S(2)}) collective-permute-start(f32[168,256]{1,0:T(8,128)S(1)} %collective-permute-done.1.d1), channel_id=1, source_target_pairs={{0,1},{1,0},{2,3},{3,2},{4,5},{5,4},{6,7},{7,6},{8,9},{9,8},{10,11... | collective-permute-start | bytes 516104 | tf_op jit(solution)/shard_map/ppermute | solution.py:263
  23.1 46.8 %copy-start.1 = (f32[2,256,256]{2,1,0:T(8,128)S(1)}, f32[2,256,256]{2,1,0:T(8,128)}, u32[]{:S(2)}) copy-start(f32[2,256,256]{2,1,0:T(8,128)} %a_ref.3) | copy-start | bytes 1572868
  23.1 5.7 %collective-permute-start.7 = (f32[168,256]{1,0:T(8,128)S(1)}, f32[168,256]{1,0:T(8,128)S(1)}, u32[]{:S(2)}, u32[]{:S(2)}) collective-permute-start(f32[168,256]{1,0:T(8,128)S(1)} %get-tuple-element.20), channel_id=1, source_target_pairs={{0,8},{1,9},{2,10},{3,11},{4,12},{5,13},{6,14},{7,15},{8,0},{9,1},... | collective-permute-start | bytes 516104 | tf_op jit(solution)/shard_map/ppermute | solution.py:261
  28.8 2.2 %collective-permute-start.8 = (f32[168,256]{1,0:T(8,128)S(1)}, f32[168,256]{1,0:T(8,128)S(1)}, u32[]{:S(2)}, u32[]{:S(2)}) collective-permute-start(f32[168,256]{1,0:T(8,128)S(1)} %collective-permute-done.7.direct_ref), channel_id=1, source_target_pairs={{0,1},{1,0},{2,3},{3,2},{4,5},{5,4},{6,7},{7,6},{8,9},{9,8},{10,11... | collective-permute-start | bytes 516104 | tf_op jit(solution)/shard_map/ppermute | solution.py:263
  31.5 10.1 %collective-permute-start.11 = (f32[168,256]{1,0:T(8,128)S(1)}, f32[168,256]{1,0:T(8,128)S(1)}, u32[]{:S(2)}, u32[]{:S(2)}) collective-permute-start(f32[168,256]{1,0:T(8,128)S(1)} %get-tuple-element.22), channel_id=1, source_target_pairs={{0,16},{1,17},{2,18},{3,19},{4,20},{5,21},{6,22},{7,23},{8,24},{9,... | collective-permute-start | bytes 516104 | tf_op jit(solution)/shard_map/ppermute | solution.py:261
  33.7 16.7 %collective-permute-start.10 = (f32[168,256]{1,0:T(8,128)S(1)}, f32[168,256]{1,0:T(8,128)S(1)}, u32[]{:S(2)}, u32[]{:S(2)}) collective-permute-start(f32[168,256]{1,0:T(8,128)S(1)} %get-tuple-element.22), channel_id=1, source_target_pairs={{0,40},{1,41},{2,42},{3,43},{4,44},{5,45},{6,46},{7,47},{8,32},{9,... | collective-permute-start | bytes 516104 | tf_op jit(solution)/shard_map/ppermute | solution.py:261
  38.2 15.3 %collective-permute-start.9 = (f32[168,256]{1,0:T(8,128)S(1)}, f32[168,256]{1,0:T(8,128)S(1)}, u32[]{:S(2)}, u32[]{:S(2)}) collective-permute-start(f32[168,256]{1,0:T(8,128)S(1)} %get-tuple-element.22), channel_id=1, source_target_pairs={{0,48},{1,49},{2,50},{3,51},{4,52},{5,53},{6,54},{7,55},{8,56},{9,... | collective-permute-start | bytes 516104 | tf_op jit(solution)/shard_map/ppermute | solution.py:261
  41.6 13.1 %collective-permute-start.14 = (f32[168,256]{1,0:T(8,128)S(1)}, f32[168,256]{1,0:T(8,128)S(1)}, u32[]{:S(2)}, u32[]{:S(2)}) collective-permute-start(f32[168,256]{1,0:T(8,128)S(1)} %collective-permute-done.11.d3), channel_id=1, source_target_pairs={{0,1},{1,0},{2,3},{3,2},{4,5},{5,4},{6,7},{7,6},{8,9},{9,8},{10,11... | collective-permute-start | bytes 516104 | tf_op jit(solution)/shard_map/ppermute | solution.py:263
  50.5 4.2 %collective-permute-start.13 = (f32[168,256]{1,0:T(8,128)S(1)}, f32[168,256]{1,0:T(8,128)S(1)}, u32[]{:S(2)}, u32[]{:S(2)}) collective-permute-start(f32[168,256]{1,0:T(8,128)S(1)} %collective-permute-done.10.d2), channel_id=1, source_target_pairs={{0,1},{1,0},{2,3},{3,2},{4,5},{5,4},{6,7},{7,6},{8,9},{9,8},{10,11... | collective-permute-start | bytes 516104 | tf_op jit(solution)/shard_map/ppermute | solution.py:263
  53.5 2.3 %collective-permute-start.12 = (f32[168,256]{1,0:T(8,128)S(1)}, f32[168,256]{1,0:T(8,128)S(1)}, u32[]{:S(2)}, u32[]{:S(2)}) collective-permute-start(f32[168,256]{1,0:T(8,128)S(1)} %collective-permute-done.9.d1), channel_id=1, source_target_pairs={{0,1},{1,0},{2,3},{3,2},{4,5},{5,4},{6,7},{7,6},{8,9},{9,8},{10,11... | collective-permute-start | bytes 516104 | tf_op jit(solution)/shard_map/ppermute | solution.py:263
  56.8 7.2 %collective-permute-start.17 = (f32[168,256]{1,0:T(8,128)S(1)}, f32[168,256]{1,0:T(8,128)S(1)}, u32[]{:S(2)}, u32[]{:S(2)}) collective-permute-start(f32[168,256]{1,0:T(8,128)S(1)} %get-tuple-element.24), channel_id=1, source_target_pairs={{0,64},{1,65},{2,66},{3,67},{4,68},{5,69},{6,70},{7,71},{8,72},{9,... | collective-permute-start | bytes 516104 | tf_op jit(solution)/shard_map/ppermute | solution.py:261
  58.3 10.4 %collective-permute-start.16 = (f32[168,256]{1,0:T(8,128)S(1)}, f32[168,256]{1,0:T(8,128)S(1)}, u32[]{:S(2)}, u32[]{:S(2)}) collective-permute-start(f32[168,256]{1,0:T(8,128)S(1)} %get-tuple-element.24), channel_id=1, source_target_pairs={{0,128},{1,129},{2,130},{3,131},{4,132},{5,133},{6,134},{7,135},{8... | collective-permute-start | bytes 516104 | tf_op jit(solution)/shard_map/ppermute | solution.py:261
  60.9 9.0 %collective-permute-start.15 = (f32[168,256]{1,0:T(8,128)S(1)}, f32[168,256]{1,0:T(8,128)S(1)}, u32[]{:S(2)}, u32[]{:S(2)}) collective-permute-start(f32[168,256]{1,0:T(8,128)S(1)} %get-tuple-element.24), channel_id=1, source_target_pairs={{0,192},{1,193},{2,194},{3,195},{4,196},{5,197},{6,198},{7,199},{8... | collective-permute-start | bytes 516104 | tf_op jit(solution)/shard_map/ppermute | solution.py:261
  63.9 8.2 %collective-permute-start.20 = (f32[168,256]{1,0:T(8,128)S(1)}, f32[168,256]{1,0:T(8,128)S(1)}, u32[]{:S(2)}, u32[]{:S(2)}) collective-permute-start(f32[168,256]{1,0:T(8,128)S(1)} %collective-permute-done.17.d3), channel_id=1, source_target_pairs={{0,1},{1,0},{2,3},{3,2},{4,5},{5,4},{6,7},{7,6},{8,9},{9,8},{10,11... | collective-permute-start | bytes 516104 | tf_op jit(solution)/shard_map/ppermute | solution.py:263
  68.7 3.4 %collective-permute-start.19 = (f32[168,256]{1,0:T(8,128)S(1)}, f32[168,256]{1,0:T(8,128)S(1)}, u32[]{:S(2)}, u32[]{:S(2)}) collective-permute-start(f32[168,256]{1,0:T(8,128)S(1)} %collective-permute-done.16.d2), channel_id=1, source_target_pairs={{0,1},{1,0},{2,3},{3,2},{4,5},{5,4},{6,7},{7,6},{8,9},{9,8},{10,11... | collective-permute-start | bytes 516104 | tf_op jit(solution)/shard_map/ppermute | solution.py:263
  70.0 2.2 %collective-permute-start.18 = (f32[168,256]{1,0:T(8,128)S(1)}, f32[168,256]{1,0:T(8,128)S(1)}, u32[]{:S(2)}, u32[]{:S(2)}) collective-permute-start(f32[168,256]{1,0:T(8,128)S(1)} %collective-permute-done.15.d1), channel_id=1, source_target_pairs={{0,1},{1,0},{2,3},{3,2},{4,5},{5,4},{6,7},{7,6},{8,9},{9,8},{10,11... | collective-permute-start | bytes 516104 | tf_op jit(solution)/shard_map/ppermute | solution.py:263
  71.3 0.9 %copy-start.2 = (f32[256]{0:T(256)S(1)}, f32[256]{0:T(256)}, u32[]{:S(2)}) copy-start(f32[256]{0:T(256)} %param.7) | copy-start | bytes 3076

commit v2 on v1

--- a/solution.py
+++ b/solution.py
@@ -39,14 +39,19 @@
 
 
 OTHER_CORE = pairs(lambda y, z, x, c: (y, z, x, 1 - c))
-X_FROM = [pairs(lambda y, z, x, c, d=d: (y, z, x - d, c)) for d in (1, 2, 3)]
-Y_FROM = [pairs(lambda y, z, x, c, d=d: (y - d, z, x, c)) for d in (1, 2, 3)]
-Z_ONE = [pairs(lambda y, z, x, c: (y, z ^ 1, x, c))]
-Z_FROM = [
-    pairs(lambda y, z, x, c: (y, z - 2, x, c)),
+X_FROM = (
+    pairs(lambda y, z, x, c: (y, z, x + (1 if c else -1), c)),
+    pairs(lambda y, z, x, c: (y, z, x + 2, c)),
+)
+Y_FROM = (
+    pairs(lambda y, z, x, c: (y + (1 if c else -1), z, x, c)),
+    pairs(lambda y, z, x, c: (y + 2, z, x, c)),
+)
+Z_ONE = pairs(lambda y, z, x, c: (y, z ^ 1, x, c))
+Z_FROM = (
+    pairs(lambda y, z, x, c: (y, z + (2 if c else -2), x, c)),
     pairs(lambda y, z, x, c: (y, z ^ 5, x, c)),
-    pairs(lambda y, z, x, c: (y, z + 2, x, c)),
-]
+)
 
 
 def split(value):
@@ -145,21 +150,22 @@
     store_half(half_ref, t_ref, core)
 
 
-def fill(slots_ref, at, core, mine_ref, direct, swapped):
+def fill(slots_ref, at, core, mine_ref, side_ref, other_side_ref, far_ref, other_far_ref):
     slots_ref[at] = mine_ref[...]
-    for d in (1, 2, 3):
-        slot = lax.rem(at + d, 4)
-        slots_ref[slot, pl.ds(pl.multiple_of(core * HALF, 8), HALF), :] = direct[d - 1][...]
-        slots_ref[slot, pl.ds(pl.multiple_of((1 - core) * HALF, 8), HALF), :] = swapped[d - 1][...]
+    slots_ref[lax.rem(at + 1 + 2 * core, 4)] = side_ref[...]
+    slots_ref[lax.rem(at + 3 - 2 * core, 4)] = other_side_ref[...]
+    far = lax.rem(at + 2, 4)
+    slots_ref[far, pl.ds(pl.multiple_of(core * HALF, 8), HALF), :] = far_ref[...]
+    slots_ref[far, pl.ds(pl.multiple_of((1 - core) * HALF, 8), HALF), :] = other_far_ref[...]
 
 
 def quad_at(axis, z, x):
     return x if axis == "x" else lax.div(z, 2)
 
 
-def quad_kernel(axis, mine_ref, d1, d2, d3, s1, s2, s3, t_ref, half_ref, slots_ref, tb_ref):
+def quad_kernel(axis, mine_ref, a, b, c, d, t_ref, half_ref, slots_ref, tb_ref):
     _, z, x, core = me()
-    fill(slots_ref, quad_at(axis, z, x), core, mine_ref, (d1, d2, d3), (s1, s2, s3))
+    fill(slots_ref, quad_at(axis, z, x), core, mine_ref, a, b, c, d)
     tb = compose(load(slots_ref.at[2]), load(slots_ref.at[3]))
     ta = compose(load(slots_ref.at[0]), load(slots_ref.at[1]))
     store(tb_ref, tb)
@@ -221,16 +227,16 @@
         out_ref[...] = w_ref[...]
 
 
-def last_kernel(scale, mine_ref, d1, d2, d3, s1, s2, s3, w_ref, end_ref, states_ref, sens_ref, slots_ref):
+def last_kernel(scale, mine_ref, a, b, c, d, w_ref, end_ref, states_ref, sens_ref, slots_ref):
     y, _, _, core = me()
-    fill(slots_ref, y, core, mine_ref, (d1, d2, d3), (s1, s2, s3))
+    fill(slots_ref, y, core, mine_ref, a, b, c, d)
     lam = end_ref[...]
     here = lam
     total = jnp.zeros((1, G), F32)
     for q in (3, 2, 1, 0):
         here = jnp.where(y == q, lam, here)
-        m, s, v, c = load(slots_ref.at[q])
-        total = total + times_row(s, lam) + c
+        m, s, v, const = load(slots_ref.at[q])
+        total = total + times_row(s, lam) + const
         lam = times_row(m, lam) + v
     sens_ref[...] = total * scale
     for state in (0, 1):
@@ -255,13 +261,13 @@
     )(*args)
 
 
-def exchange(half, moves):
-    direct, swapped = [], []
-    for move in moves:
-        direct.append(lax.ppermute(half, "tm", move))
-    for part in direct:
-        swapped.append(lax.ppermute(part, "tm", OTHER_CORE))
-    return direct, swapped
+def send(value, move):
+    return lax.ppermute(value, "tm", move)
+
+
+def gather(whole, half, moves):
+    side, far = send(whole, moves[0]), send(half, moves[1])
+    return side, send(side, OTHER_CORE), far, send(far, OTHER_CORE)
 
 
 def local(step_ops, sources, terminal, inertia_jac, gen_bus):
@@ -273,32 +279,33 @@
     )
     (leaf,) = call(leaf_kernel, [t], [step_ops, rows])
     total = leaf
-    other = lax.ppermute(total, "tm", OTHER_CORE)
+    other = send(total, OTHER_CORE)
     total, half = call(core_kernel, [t, h], [total, other])
 
-    direct, swapped = exchange(half, X_FROM)
+    parts = gather(total, half, X_FROM)
     (own,) = call(own_core_kernel, [w], [leaf, step_ops, rows, other], scratch=[pltpu.VMEM(w, F32)])
     total, half, slots, tb = call(
-        part(quad_kernel, "x"), [t, h, (4,) + t, t], [total, *direct, *swapped], products=3
-    )
-
-    direct, swapped = exchange(half, Z_ONE)
+        part(quad_kernel, "x"), [t, h, (4,) + t, t], [total, *parts], products=3
+    )
+
+    direct = send(half, Z_ONE)
+    swapped = send(direct, OTHER_CORE)
     (own,) = call(part(own_quad_kernel, "x"), [w], [own, slots, tb], products=2)
-    total, half, late = call(pair_kernel, [t, h, t], [total, *direct, *swapped])
-
-    direct, swapped = exchange(half, Z_FROM)
+    total, half, late = call(pair_kernel, [t, h, t], [total, direct, swapped])
+
+    parts = gather(total, half, Z_FROM)
     (own,) = call(own_pair_kernel, [w], [own, late])
     total, half, slots, tb = call(
-        part(quad_kernel, "z"), [t, h, (4,) + t, t], [total, *direct, *swapped], products=3
-    )
-
-    direct, swapped = exchange(half, Y_FROM)
+        part(quad_kernel, "z"), [t, h, (4,) + t, t], [total, *parts], products=3
+    )
+
+    parts = gather(total, half, Y_FROM)
     (own,) = call(part(own_quad_kernel, "z"), [w], [own, slots, tb], products=2)
     steps = step_ops.shape[0] * lax.axis_size("tm")
     states, sens = call(
         part(last_kernel, float(steps) ** -0.5),
         [(2, N), (1, G)],
-        [total, *direct, *swapped, own, terminal.reshape(1, N)],
+        [total, *parts, own, terminal.reshape(1, N)],
         scratch=[pltpu.VMEM((4,) + t, F32)],
     )
     return states, sens.reshape(G)

time: 73.6 us -> 70.6 us (0.959)
  starting transfers between devices: 34.1 us -> 31.7 us
  waiting for transfers between devices: 29.2 us -> 28.4 us
    ppermute x21 -> x15, starting transfers between devices: 34.1 us -> 31.7 us  [send(): return lax.ppermute(value, 'tm', move)]
    ppermute x21 -> x15, waiting for transfers between devices: 29.2 us -> 28.4 us  [send(): return lax.ppermute(value, 'tm', move)]
  transfers between devices with their start and end apart: 21 -> 15, of which waited for: 13 -> 10; matrix products, arithmetic and copies ran while one was open for 0% -> 0% of each run, Pallas kernels for 3% -> 3%
where the time goes in v2:
time: 70.6 us; the launch traced here: 70.4 us
  starting transfers between devices  31.7 us (45%)
  waiting for transfers between devices  28.4 us (40%)
  Pallas kernels  6.95 us (10%)
  other arithmetic  1.43 us (2%)
  local copies, waits for them, and re-layouts  1.13 us (2%)
  between operations  0.75 us (1%)
    ppermute x15, starting transfers between devices, send(): return lax.ppermute(value, 'tm', move)  31.7 us
    ppermute x15, waiting for transfers between devices, send(): return lax.ppermute(value, 'tm', move)  28.4 us
    pallas_call x10, Pallas kernels, call(): pl.pallas_call(kernel, out_shape=shapes, in_specs=[VM] * len(args), out_s...  6.95 us
  transfers between devices with their start and end apart: 15, of which 10 were waited for; matrix products, arithmetic and copies ran while one was open for 0% of the time, Pallas kernels for 3%

profile of v2, /device:TPU:1, one launch (start us, length us, event | category | flops | bytes accessed | tf_op | source)
XLA Modules:
  0.0 70.4 jit_solution(7068680256906271047)
XLA Ops:
  0.6 0.7 convert_bitcast_fusion
  1.4 0.8 %fusion.row_ref = f32[8,256]{1,0:T(8,128)S(1)} fusion(f32[1,64]{1,0:T(1,128)S(1)} %convert_bitcast_fusion, f32[2,64]{1,0:T(2,128)} %param.8, f32[2,256]{1,0:T(2,128)} %param.6, f32[8]{0:T(128)S(1)} %pad.13.clone), kind=kLoop, calls=%fused_computation.5 | loop fusion | flops 22528 | bytes 11040 | tf_op jit(solution)/shard_map/concatenate | solution.py:277
  2.1 1.0 %copy-done = f32[2,256,256]{2,1,0:T(8,128)S(1)} copy-done((f32[2,256,256]{2,1,0:T(8,128)S(1)}, f32[2,256,256]{2,1,0:T(8,128)}, u32[]{:S(2)}) %copy-start) | copy-done | bytes 524312
  3.2 0.6 shard_map.68.mine_ref.t_ref
  3.7 3.3 %collective-permute-start = (f32[336,256]{1,0:T(8,128)S(1)}, f32[336,256]{1,0:T(8,128)S(1)}, u32[]{:S(2)}, u32[]{:S(2)}) collective-permute-start(f32[336,256]{1,0:T(8,128)S(1)} %shard_map.68.mine_ref.t_ref), channel_id=1, source_target_pairs={{0,1},{1,0},{2,3},{3,2},{4,5},{5,4},{6,7},{7,6},{8,9},{9,8},{10,11... | collective-permute-start | bytes 1032200 | tf_op jit(solution)/shard_map/ppermute | solution.py:265
  7.0 1.3 %collective-permute-done.other_ref = f32[336,256]{1,0:T(8,128)S(1)} collective-permute-done((f32[336,256]{1,0:T(8,128)S(1)}, f32[336,256]{1,0:T(8,128)S(1)}, u32[]{:S(2)}, u32[]{:S(2)}) %collective-permute-start) | collective-permute-done | bytes 344096 | tf_op jit(solution)/shard_map/ppermute | solution.py:265
  8.8 1.9 %collective-permute-start.3 = (f32[168,256]{1,0:T(8,128)S(1)}, f32[168,256]{1,0:T(8,128)S(1)}, u32[]{:S(2)}, u32[]{:S(2)}) collective-permute-start(f32[168,256]{1,0:T(8,128)S(1)} %get-tuple-element.18), channel_id=1, source_target_pairs={{0,4},{1,5},{2,6},{3,7},{4,0},{5,1},{6,2},{7,3},{8,12},{9,13},{10,... | collective-permute-start | bytes 516104 | tf_op jit(solution)/shard_map/ppermute | solution.py:265
  10.7 9.0 %collective-permute-done.1.a = f32[336,256]{1,0:T(8,128)S(1)} collective-permute-done((f32[336,256]{1,0:T(8,128)S(1)}, f32[336,256]{1,0:T(8,128)S(1)}, u32[]{:S(2)}, u32[]{:S(2)}) %collective-permute-start.1) | collective-permute-done | bytes 344096 | tf_op jit(solution)/shard_map/ppermute | solution.py:265
  19.8 0.5 collective-permute-start.4
  20.3 1.4 %collective-permute-done.4.d = f32[168,256]{1,0:T(8,128)S(1)} collective-permute-done((f32[168,256]{1,0:T(8,128)S(1)}, f32[168,256]{1,0:T(8,128)S(1)}, u32[]{:S(2)}, u32[]{:S(2)}) %collective-permute-start.4) | collective-permute-done | bytes 172064 | tf_op jit(solution)/shard_map/ppermute | solution.py:265
  21.7 1.0 %shard_map.70 = (f32[336,256]{1,0:T(8,128)S(1)}, f32[168,256]{1,0:T(8,128)S(1)}, f32[4,336,256]{2,1,0:T(8,128)S(1)}, f32[336,256]{1,0:T(8,128)S(1)}) custom-call(f32[336,256]{1,0:T(8,128)S(1)} %get-tuple-element.17.mine_ref, f32[336,256]{1,0:T(8,128)S(1)} %collective-permute-done.1.a, f32[336,256]{1,0:T(8,128)S(1)} %collective-permute-done.2.b, ...), custom_call_target="tpu_custom_call" | custom-call | flops 377487360 | bytes 1048576 | tf_op jit(solution)/shard_map/pallas_call | solution.py:251
  22.7 0.5 collective-permute-start.5
  23.2 5.4 %collective-permute-done.5.direct_ref = f32[168,256]{1,0:T(8,128)S(1)} collective-permute-done((f32[168,256]{1,0:T(8,128)S(1)}, f32[168,256]{1,0:T(8,128)S(1)}, u32[]{:S(2)}, u32[]{:S(2)}) %collective-permute-start.5) | collective-permute-done | bytes 172064 | tf_op jit(solution)/shard_map/ppermute | solution.py:265
  28.6 1.0 %collective-permute-start.6 = (f32[168,256]{1,0:T(8,128)S(1)}, f32[168,256]{1,0:T(8,128)S(1)}, u32[]{:S(2)}, u32[]{:S(2)}) collective-permute-start(f32[168,256]{1,0:T(8,128)S(1)} %collective-permute-done.5.direct_ref), channel_id=1, source_target_pairs={{0,1},{1,0},{2,3},{3,2},{4,5},{5,4},{6,7},{7,6},{8,9},{9,8},{10,11... | collective-permute-start | bytes 516104 | tf_op jit(solution)/shard_map/ppermute | solution.py:265
  29.6 1.0 %collective-permute-done.6.swapped_ref = f32[168,256]{1,0:T(8,128)S(1)} collective-permute-done((f32[168,256]{1,0:T(8,128)S(1)}, f32[168,256]{1,0:T(8,128)S(1)}, u32[]{:S(2)}, u32[]{:S(2)}) %collective-permute-start.6) | collective-permute-done | bytes 172064 | tf_op jit(solution)/shard_map/ppermute | solution.py:265
  30.6 0.4 shard_map.71
  31.0 2.0 %collective-permute-start.7 = (f32[336,256]{1,0:T(8,128)S(1)}, f32[336,256]{1,0:T(8,128)S(1)}, u32[]{:S(2)}, u32[]{:S(2)}) collective-permute-start(f32[336,256]{1,0:T(8,128)S(1)} %get-tuple-element.21.mine_ref), channel_id=1, source_target_pairs={{0,48},{1,17},{2,50},{3,19},{4,52},{5,21},{6,54},{7,23},{8,56},{9,... | collective-permute-start | bytes 1032200 | tf_op jit(solution)/shard_map/ppermute | solution.py:265
  33.0 4.5 %collective-permute-start.9 = (f32[168,256]{1,0:T(8,128)S(1)}, f32[168,256]{1,0:T(8,128)S(1)}, u32[]{:S(2)}, u32[]{:S(2)}) collective-permute-start(f32[168,256]{1,0:T(8,128)S(1)} %get-tuple-element.22), channel_id=1, source_target_pairs={{0,40},{1,41},{2,42},{3,43},{4,44},{5,45},{6,46},{7,47},{8,32},{9,... | collective-permute-start | bytes 516104 | tf_op jit(solution)/shard_map/ppermute | solution.py:265
  37.5 4.6 %collective-permute-done.7.a = f32[336,256]{1,0:T(8,128)S(1)} collective-permute-done((f32[336,256]{1,0:T(8,128)S(1)}, f32[336,256]{1,0:T(8,128)S(1)}, u32[]{:S(2)}, u32[]{:S(2)}) %collective-permute-start.7) | collective-permute-done | bytes 344096 | tf_op jit(solution)/shard_map/ppermute | solution.py:265
  42.1 8.4 %collective-permute-start.8 = (f32[336,256]{1,0:T(8,128)S(1)}, f32[336,256]{1,0:T(8,128)S(1)}, u32[]{:S(2)}, u32[]{:S(2)}) collective-permute-start(f32[336,256]{1,0:T(8,128)S(1)} %collective-permute-done.7.a), channel_id=1, source_target_pairs={{0,1},{1,0},{2,3},{3,2},{4,5},{5,4},{6,7},{7,6},{8,9},{9,8},{10,11... | collective-permute-start | bytes 1032200 | tf_op jit(solution)/shard_map/ppermute | solution.py:265
  50.5 0.5 collective-permute-done.9.c
  51.1 1.3 %collective-permute-start.10 = (f32[168,256]{1,0:T(8,128)S(1)}, f32[168,256]{1,0:T(8,128)S(1)}, u32[]{:S(2)}, u32[]{:S(2)}) collective-permute-start(f32[168,256]{1,0:T(8,128)S(1)} %collective-permute-done.9.c), channel_id=1, source_target_pairs={{0,1},{1,0},{2,3},{3,2},{4,5},{5,4},{6,7},{7,6},{8,9},{9,8},{10,11... | collective-permute-start | bytes 516104 | tf_op jit(solution)/shard_map/ppermute | solution.py:265
  52.4 1.0 %collective-permute-done.10.d = f32[168,256]{1,0:T(8,128)S(1)} collective-permute-done((f32[168,256]{1,0:T(8,128)S(1)}, f32[168,256]{1,0:T(8,128)S(1)}, u32[]{:S(2)}, u32[]{:S(2)}) %collective-permute-start.10) | collective-permute-done | bytes 172064 | tf_op jit(solution)/shard_map/ppermute | solution.py:265
  53.4 1.0 %shard_map.72 = (f32[336,256]{1,0:T(8,128)S(1)}, f32[168,256]{1,0:T(8,128)S(1)}, f32[4,336,256]{2,1,0:T(8,128)S(1)}, f32[336,256]{1,0:T(8,128)S(1)}) custom-call(f32[336,256]{1,0:T(8,128)S(1)} %get-tuple-element.21.mine_ref, f32[336,256]{1,0:T(8,128)S(1)} %collective-permute-done.7.a, f32[336,256]{1,0:T(8,128)S(1)} %collective-permute-done.8.b, ...), custom_call_target="tpu_custom_call" | custom-call | flops 377487360 | bytes 1048576 | tf_op jit(solution)/shard_map/pallas_call | solution.py:251
  54.4 1.4 %collective-permute-start.11 = (f32[336,256]{1,0:T(8,128)S(1)}, f32[336,256]{1,0:T(8,128)S(1)}, u32[]{:S(2)}, u32[]{:S(2)}) collective-permute-start(f32[336,256]{1,0:T(8,128)S(1)} %get-tuple-element.23.mine_ref), channel_id=1, source_target_pairs={{0,192},{1,65},{2,194},{3,67},{4,196},{5,69},{6,198},{7,71},{8,200... | collective-permute-start | bytes 1032200 | tf_op jit(solution)/shard_map/ppermute | solution.py:265
  55.8 2.6 %collective-permute-start.13 = (f32[168,256]{1,0:T(8,128)S(1)}, f32[168,256]{1,0:T(8,128)S(1)}, u32[]{:S(2)}, u32[]{:S(2)}) collective-permute-start(f32[168,256]{1,0:T(8,128)S(1)} %get-tuple-element.24), channel_id=1, source_target_pairs={{0,128},{1,129},{2,130},{3,131},{4,132},{5,133},{6,134},{7,135},{8... | collective-permute-start | bytes 516104 | tf_op jit(solution)/shard_map/ppermute | solution.py:265
  58.4 3.5 %collective-permute-done.11.a = f32[336,256]{1,0:T(8,128)S(1)} collective-permute-done((f32[336,256]{1,0:T(8,128)S(1)}, f32[336,256]{1,0:T(8,128)S(1)}, u32[]{:S(2)}, u32[]{:S(2)}) %collective-permute-start.11) | collective-permute-done | bytes 344096 | tf_op jit(solution)/shard_map/ppermute | solution.py:265
  61.9 4.2 %collective-permute-start.12 = (f32[336,256]{1,0:T(8,128)S(1)}, f32[336,256]{1,0:T(8,128)S(1)}, u32[]{:S(2)}, u32[]{:S(2)}) collective-permute-start(f32[336,256]{1,0:T(8,128)S(1)} %collective-permute-done.11.a), channel_id=1, source_target_pairs={{0,1},{1,0},{2,3},{3,2},{4,5},{5,4},{6,7},{7,6},{8,9},{9,8},{10,11... | collective-permute-start | bytes 1032200 | tf_op jit(solution)/shard_map/ppermute | solution.py:265
  66.1 0.6 collective-permute-done.13.c
  67.0 0.8 %shard_map.74.w_ref = f32[528,256]{1,0:T(8,128)S(1)} custom-call(f32[528,256]{1,0:T(8,128)S(1)} %shard_map.73.w_ref, f32[4,336,256]{2,1,0:T(8,128)S(1)} %get-tuple-element.25.slots_ref, f32[336,256]{1,0:T(8,128)S(1)} %get-tuple-element.26.tb_ref), custom_call_target="tpu_custom_call" | custom-call | flops 251658240 | bytes 1048576 | tf_op jit(solution)/shard_map/pallas_call | solution.py:251
  68.2 0.8 %shard_map.76.w_ref = f32[528,256]{1,0:T(8,128)S(1)} custom-call(f32[528,256]{1,0:T(8,128)S(1)} %shard_map.75.w_ref, f32[4,336,256]{2,1,0:T(8,128)S(1)} %get-tuple-element.28.slots_ref, f32[336,256]{1,0:T(8,128)S(1)} %get-tuple-element.29.tb_ref), custom_call_target="tpu_custom_call" | custom-call | flops 251658240 | bytes 1048576 | tf_op jit(solution)/shard_map/pallas_call | solution.py:251
  69.1 1.3 %shard_map.77 = (f32[2,256]{1,0:T(2,128)}, f32[1,64]{1,0:T(1,128)}) custom-call(f32[336,256]{1,0:T(8,128)S(1)} %get-tuple-element.23.mine_ref, f32[336,256]{1,0:T(8,128)S(1)} %collective-permute-done.11.a, f32[336,256]{1,0:T(8,128)S(1)} %collective-permute-done.12.b, f32[168,256]{1,0:T(8,128)S(1)} %collective-permute-done.13.c, ...), custom_call_target="tpu_custom_call" | custom-call | flops 125829120 | bytes 1048576 | tf_op jit(solution)/shard_map/pallas_call | solution.py:251
  (18 shorter events, 1.2 us)
Async XLA Ops:
  2.1 1.0 %copy-start = (f32[2,256,256]{2,1,0:T(8,128)S(1)}, f32[2,256,256]{2,1,0:T(8,128)}, u32[]{:S(2)}) copy-start(f32[2,256,256]{2,1,0:T(8,128)} %a_ref.3) | copy-start | bytes 1572868
  3.7 4.6 %collective-permute-start = (f32[336,256]{1,0:T(8,128)S(1)}, f32[336,256]{1,0:T(8,128)S(1)}, u32[]{:S(2)}, u32[]{:S(2)}) collective-permute-start(f32[336,256]{1,0:T(8,128)S(1)} %shard_map.68.mine_ref.t_ref), channel_id=1, source_target_pairs={{0,1},{1,0},{2,3},{3,2},{4,5},{5,4},{6,7},{7,6},{8,9},{9,8},{10,11... | collective-permute-start | bytes 1032200 | tf_op jit(solution)/shard_map/ppermute | solution.py:265
  8.7 11.1 %collective-permute-start.1 = (f32[336,256]{1,0:T(8,128)S(1)}, f32[336,256]{1,0:T(8,128)S(1)}, u32[]{:S(2)}, u32[]{:S(2)}) collective-permute-start(f32[336,256]{1,0:T(8,128)S(1)} %get-tuple-element.17.mine_ref), channel_id=1, source_target_pairs={{0,6},{1,3},{2,0},{3,5},{4,2},{5,7},{6,4},{7,1},{8,14},{9,11},{10,... | collective-permute-start | bytes 1032200 | tf_op jit(solution)/shard_map/ppermute | solution.py:265
  8.8 11.0 %collective-permute-start.3 = (f32[168,256]{1,0:T(8,128)S(1)}, f32[168,256]{1,0:T(8,128)S(1)}, u32[]{:S(2)}, u32[]{:S(2)}) collective-permute-start(f32[168,256]{1,0:T(8,128)S(1)} %get-tuple-element.18), channel_id=1, source_target_pairs={{0,4},{1,5},{2,6},{3,7},{4,0},{5,1},{6,2},{7,3},{8,12},{9,13},{10,... | collective-permute-start | bytes 516104 | tf_op jit(solution)/shard_map/ppermute | solution.py:265
  19.8 1.9 %collective-permute-start.2 = (f32[336,256]{1,0:T(8,128)S(1)}, f32[336,256]{1,0:T(8,128)S(1)}, u32[]{:S(2)}, u32[]{:S(2)}) collective-permute-start(f32[336,256]{1,0:T(8,128)S(1)} %collective-permute-done.1.a), channel_id=1, source_target_pairs={{0,1},{1,0},{2,3},{3,2},{4,5},{5,4},{6,7},{7,6},{8,9},{9,8},{10,11... | collective-permute-start | bytes 1032200 | tf_op jit(solution)/shard_map/ppermute | solution.py:265
  19.8 1.9 %collective-permute-start.4 = (f32[168,256]{1,0:T(8,128)S(1)}, f32[168,256]{1,0:T(8,128)S(1)}, u32[]{:S(2)}, u32[]{:S(2)}) collective-permute-start(f32[168,256]{1,0:T(8,128)S(1)} %collective-permute-done.3.c), channel_id=1, source_target_pairs={{0,1},{1,0},{2,3},{3,2},{4,5},{5,4},{6,7},{7,6},{8,9},{9,8},{10,11... | collective-permute-start | bytes 516104 | tf_op jit(solution)/shard_map/ppermute | solution.py:265
  22.7 44.1 %copy-start.1 = (f32[2,256,256]{2,1,0:T(8,128)S(1)}, f32[2,256,256]{2,1,0:T(8,128)}, u32[]{:S(2)}) copy-start(f32[2,256,256]{2,1,0:T(8,128)} %a_ref.3) | copy-start | bytes 1572868
  22.7 5.9 %collective-permute-start.5 = (f32[168,256]{1,0:T(8,128)S(1)}, f32[168,256]{1,0:T(8,128)S(1)}, u32[]{:S(2)}, u32[]{:S(2)}) collective-permute-start(f32[168,256]{1,0:T(8,128)S(1)} %get-tuple-element.20), channel_id=1, source_target_pairs={{0,8},{1,9},{2,10},{3,11},{4,12},{5,13},{6,14},{7,15},{8,0},{9,1},... | collective-permute-start | bytes 516104 | tf_op jit(solution)/shard_map/ppermute | solution.py:265
  28.6 2.0 %collective-permute-start.6 = (f32[168,256]{1,0:T(8,128)S(1)}, f32[168,256]{1,0:T(8,128)S(1)}, u32[]{:S(2)}, u32[]{:S(2)}) collective-permute-start(f32[168,256]{1,0:T(8,128)S(1)} %collective-permute-done.5.direct_ref), channel_id=1, source_target_pairs={{0,1},{1,0},{2,3},{3,2},{4,5},{5,4},{6,7},{7,6},{8,9},{9,8},{10,11... | collective-permute-start | bytes 516104 | tf_op jit(solution)/shard_map/ppermute | solution.py:265
  31.0 11.1 %collective-permute-start.7 = (f32[336,256]{1,0:T(8,128)S(1)}, f32[336,256]{1,0:T(8,128)S(1)}, u32[]{:S(2)}, u32[]{:S(2)}) collective-permute-start(f32[336,256]{1,0:T(8,128)S(1)} %get-tuple-element.21.mine_ref), channel_id=1, source_target_pairs={{0,48},{1,17},{2,50},{3,19},{4,52},{5,21},{6,54},{7,23},{8,56},{9,... | collective-permute-start | bytes 1032200 | tf_op jit(solution)/shard_map/ppermute | solution.py:265
  33.0 18.0 %collective-permute-start.9 = (f32[168,256]{1,0:T(8,128)S(1)}, f32[168,256]{1,0:T(8,128)S(1)}, u32[]{:S(2)}, u32[]{:S(2)}) collective-permute-start(f32[168,256]{1,0:T(8,128)S(1)} %get-tuple-element.22), channel_id=1, source_target_pairs={{0,40},{1,41},{2,42},{3,43},{4,44},{5,45},{6,46},{7,47},{8,32},{9,... | collective-permute-start | bytes 516104 | tf_op jit(solution)/shard_map/ppermute | solution.py:265
  42.1 11.3 %collective-permute-start.8 = (f32[336,256]{1,0:T(8,128)S(1)}, f32[336,256]{1,0:T(8,128)S(1)}, u32[]{:S(2)}, u32[]{:S(2)}) collective-permute-start(f32[336,256]{1,0:T(8,128)S(1)} %collective-permute-done.7.a), channel_id=1, source_target_pairs={{0,1},{1,0},{2,3},{3,2},{4,5},{5,4},{6,7},{7,6},{8,9},{9,8},{10,11... | collective-permute-start | bytes 1032200 | tf_op jit(solution)/shard_map/ppermute | solution.py:265
  51.1 2.3 %collective-permute-start.10 = (f32[168,256]{1,0:T(8,128)S(1)}, f32[168,256]{1,0:T(8,128)S(1)}, u32[]{:S(2)}, u32[]{:S(2)}) collective-permute-start(f32[168,256]{1,0:T(8,128)S(1)} %collective-permute-done.9.c), channel_id=1, source_target_pairs={{0,1},{1,0},{2,3},{3,2},{4,5},{5,4},{6,7},{7,6},{8,9},{9,8},{10,11... | collective-permute-start | bytes 516104 | tf_op jit(solution)/shard_map/ppermute | solution.py:265
  54.4 7.5 %collective-permute-start.11 = (f32[336,256]{1,0:T(8,128)S(1)}, f32[336,256]{1,0:T(8,128)S(1)}, u32[]{:S(2)}, u32[]{:S(2)}) collective-permute-start(f32[336,256]{1,0:T(8,128)S(1)} %get-tuple-element.23.mine_ref), channel_id=1, source_target_pairs={{0,192},{1,65},{2,194},{3,67},{4,196},{5,69},{6,198},{7,71},{8,200... | collective-permute-start | bytes 1032200 | tf_op jit(solution)/shard_map/ppermute | solution.py:265
  55.8 10.9 %collective-permute-start.13 = (f32[168,256]{1,0:T(8,128)S(1)}, f32[168,256]{1,0:T(8,128)S(1)}, u32[]{:S(2)}, u32[]{:S(2)}) collective-permute-start(f32[168,256]{1,0:T(8,128)S(1)} %get-tuple-element.24), channel_id=1, source_target_pairs={{0,128},{1,129},{2,130},{3,131},{4,132},{5,133},{6,134},{7,135},{8... | collective-permute-start | bytes 516104 | tf_op jit(solution)/shard_map/ppermute | solution.py:265
  61.9 7.2 %collective-permute-start.12 = (f32[336,256]{1,0:T(8,128)S(1)}, f32[336,256]{1,0:T(8,128)S(1)}, u32[]{:S(2)}, u32[]{:S(2)}) collective-permute-start(f32[336,256]{1,0:T(8,128)S(1)} %collective-permute-done.11.a), channel_id=1, source_target_pairs={{0,1},{1,0},{2,3},{3,2},{4,5},{5,4},{6,7},{7,6},{8,9},{9,8},{10,11... | collective-permute-start | bytes 1032200 | tf_op jit(solution)/shard_map/ppermute | solution.py:265
  66.7 2.3 %collective-permute-start.14 = (f32[168,256]{1,0:T(8,128)S(1)}, f32[168,256]{1,0:T(8,128)S(1)}, u32[]{:S(2)}, u32[]{:S(2)}) collective-permute-start(f32[168,256]{1,0:T(8,128)S(1)} %collective-permute-done.13.c), channel_id=1, source_target_pairs={{0,1},{1,0},{2,3},{3,2},{4,5},{5,4},{6,7},{7,6},{8,9},{9,8},{10,11... | collective-permute-start | bytes 516104 | tf_op jit(solution)/shard_map/ppermute | solution.py:265
  68.2 0.9 %copy-start.2 = (f32[256]{0:T(256)S(1)}, f32[256]{0:T(256)}, u32[]{:S(2)}) copy-start(f32[256]{0:T(256)} %param.7) | copy-start | bytes 3076

commit v3 on v2

--- a/solution.py
+++ b/solution.py
@@ -16,6 +16,8 @@
 C = MS + 8
 ROWS = MS + 16
 HALF = ROWS // 2
+QUARTER = 88
+MEET = HALF - QUARTER
 W_ROWS = 2 * N + 16
 F32 = jnp.float32
 VM = pl.BlockSpec(memory_space=pltpu.VMEM)
@@ -48,10 +50,8 @@
     pairs(lambda y, z, x, c: (y + 2, z, x, c)),
 )
 Z_ONE = pairs(lambda y, z, x, c: (y, z ^ 1, x, c))
-Z_FROM = (
-    pairs(lambda y, z, x, c: (y, z + (2 if c else -2), x, c)),
-    pairs(lambda y, z, x, c: (y, z ^ 5, x, c)),
-)
+Z_SIDE = pairs(lambda y, z, x, c: (y, z + (1 if z % 2 else -1), x, c))
+Z_FAR = pairs(lambda y, z, x, c: (y, z ^ 5, x, c))
 
 
 def split(value):
@@ -140,7 +140,7 @@
     store_half(half_ref, t_ref, core)
 
 
-def pair_kernel(mine_ref, direct_ref, swapped_ref, t_ref, half_ref, other_ref):
+def pair_kernel(mine_ref, direct_ref, swapped_ref, t_ref, half_ref, quarter_ref, other_ref):
     _, z, _, core = me()
     other_ref[pl.ds(pl.multiple_of(core * HALF, 8), HALF), :] = direct_ref[...]
     other_ref[pl.ds(pl.multiple_of((1 - core) * HALF, 8), HALF), :] = swapped_ref[...]
@@ -148,6 +148,25 @@
     early, late = pick(first, load(mine_ref), load(other_ref))
     store(t_ref, compose(early, late))
     store_half(half_ref, t_ref, core)
+    at = core * HALF + (1 - lax.rem(z, 2)) * MEET
+    quarter_ref[...] = t_ref[pl.ds(pl.multiple_of(at, 8), QUARTER), :]
+
+
+def fill_z(slots_ref, z, core, mine_ref, own_ref, got_ref, own_other_ref, got_other_ref):
+    at, odd = lax.div(z, 2), lax.rem(z, 2)
+    slots_ref[at] = mine_ref[...]
+    far = lax.rem(at + 2, 4)
+    for ref, parity, half in (
+        (own_ref, odd, core),
+        (got_ref, 1 - odd, core),
+        (own_other_ref, odd, 1 - core),
+        (got_other_ref, 1 - odd, 1 - core),
+    ):
+        side = lax.rem(at + 3 - 2 * parity, 4)
+        row = half * HALF
+        slots_ref[side, pl.ds(pl.multiple_of(row, 8), HALF), :] = ref[0:HALF, :]
+        row = row + parity * MEET
+        slots_ref[far, pl.ds(pl.multiple_of(row, 8), QUARTER), :] = ref[HALF : HALF + QUARTER, :]
 
 
 def fill(slots_ref, at, core, mine_ref, side_ref, other_side_ref, far_ref, other_far_ref):
@@ -165,7 +184,10 @@
 
 def quad_kernel(axis, mine_ref, a, b, c, d, t_ref, half_ref, slots_ref, tb_ref):
     _, z, x, core = me()
-    fill(slots_ref, quad_at(axis, z, x), core, mine_ref, a, b, c, d)
+    if axis == "x":
+        fill(slots_ref, x, core, mine_ref, a, b, c, d)
+    else:
+        fill_z(slots_ref, z, core, mine_ref, a, b, c, d)
     tb = compose(load(slots_ref.at[2]), load(slots_ref.at[3]))
     ta = compose(load(slots_ref.at[0]), load(slots_ref.at[1]))
     store(tb_ref, tb)
@@ -291,9 +313,14 @@
     direct = send(half, Z_ONE)
     swapped = send(direct, OTHER_CORE)
     (own,) = call(part(own_quad_kernel, "x"), [w], [own, slots, tb], products=2)
-    total, half, late = call(pair_kernel, [t, h, t], [total, direct, swapped])
-
-    parts = gather(total, half, Z_FROM)
+    total, half, quarter, late = call(
+        pair_kernel, [t, h, (QUARTER, N), t], [total, direct, swapped]
+    )
+
+    far, side = send(quarter, Z_FAR), send(half, Z_SIDE)
+    mine = jnp.concatenate([side, far])
+    got = send(mine, Z_ONE)
+    parts = mine, got, send(mine, OTHER_CORE), send(got, OTHER_CORE)
     (own,) = call(own_pair_kernel, [w], [own, late])
     total, half, slots, tb = call(
         part(quad_kernel, "z"), [t, h, (4,) + t, t], [total, *parts], products=3

time: 70.6 us -> 70.1 us (level)
  starting transfers between devices: 31.7 us -> 27.4 us
  waiting for transfers between devices: 28.4 us -> 32.5 us
    ppermute x15 -> x16, starting transfers between devices: 31.7 us -> 27.4 us  [send(): return lax.ppermute(value, 'tm', move)]
    ppermute x15 -> x16, waiting for transfers between devices: 28.4 us -> 32.5 us  [send(): return lax.ppermute(value, 'tm', move)]
  transfers between devices with their start and end apart: 15 -> 16, of which waited for: 10 -> 11; matrix products, arithmetic and copies ran while one was open for 0% -> 0% of each run, Pallas kernels for 3% -> 3%
where the time goes in v3:
time: 70.1 us; the launch traced here: 70 us
  waiting for transfers between devices  32.5 us (46%)
  starting transfers between devices  27.4 us (39%)
  Pallas kernels  6.78 us (10%)
  other arithmetic  1.43 us (2%)
  local copies, waits for them, and re-layouts  1.15 us (2%)
  between operations  0.76 us (1%)
    ppermute x16, waiting for transfers between devices, send(): return lax.ppermute(value, 'tm', move)  32.5 us
    ppermute x16, starting transfers between devices, send(): return lax.ppermute(value, 'tm', move)  27.4 us
    pallas_call x10, Pallas kernels, call(): pl.pallas_call(kernel, out_shape=shapes, in_specs=[VM] * len(args), out_s...  6.78 us
  transfers between devices with their start and end apart: 16, of which 11 were waited for; matrix products, arithmetic and copies ran while one was open for 0% of the time, Pallas kernels for 3%

profile of v3, /device:TPU:1, one launch (start us, length us, event | category | flops | bytes accessed | tf_op | source)
XLA Modules:
  0.0 70.0 jit_solution(6129541497916664911)
XLA Ops:
  0.6 0.7 convert_bitcast_fusion
  1.4 0.8 %fusion.row_ref = f32[8,256]{1,0:T(8,128)S(1)} fusion(f32[1,64]{1,0:T(1,128)S(1)} %convert_bitcast_fusion, f32[2,64]{1,0:T(2,128)} %param.8, f32[2,256]{1,0:T(2,128)} %param.6, f32[8]{0:T(128)S(1)} %pad.13.clone), kind=kLoop, calls=%fused_computation.5 | loop fusion | flops 22528 | bytes 11040 | tf_op jit(solution)/shard_map/concatenate | solution.py:299
  2.1 1.0 %copy-done = f32[2,256,256]{2,1,0:T(8,128)S(1)} copy-done((f32[2,256,256]{2,1,0:T(8,128)S(1)}, f32[2,256,256]{2,1,0:T(8,128)}, u32[]{:S(2)}) %copy-start) | copy-done | bytes 524312
  3.2 0.6 shard_map.68.mine_ref.t_ref
  3.7 3.3 %collective-permute-start = (f32[336,256]{1,0:T(8,128)S(1)}, f32[336,256]{1,0:T(8,128)S(1)}, u32[]{:S(2)}, u32[]{:S(2)}) collective-permute-start(f32[336,256]{1,0:T(8,128)S(1)} %shard_map.68.mine_ref.t_ref), channel_id=1, source_target_pairs={{0,1},{1,0},{2,3},{3,2},{4,5},{5,4},{6,7},{7,6},{8,9},{9,8},{10,11... | collective-permute-start | bytes 1032200 | tf_op jit(solution)/shard_map/ppermute | solution.py:287
  7.0 1.3 %collective-permute-done.other_ref = f32[336,256]{1,0:T(8,128)S(1)} collective-permute-done((f32[336,256]{1,0:T(8,128)S(1)}, f32[336,256]{1,0:T(8,128)S(1)}, u32[]{:S(2)}, u32[]{:S(2)}) %collective-permute-start) | collective-permute-done | bytes 344096 | tf_op jit(solution)/shard_map/ppermute | solution.py:287
  8.8 1.9 %collective-permute-start.3 = (f32[168,256]{1,0:T(8,128)S(1)}, f32[168,256]{1,0:T(8,128)S(1)}, u32[]{:S(2)}, u32[]{:S(2)}) collective-permute-start(f32[168,256]{1,0:T(8,128)S(1)} %get-tuple-element.19), channel_id=1, source_target_pairs={{0,4},{1,5},{2,6},{3,7},{4,0},{5,1},{6,2},{7,3},{8,12},{9,13},{10,... | collective-permute-start | bytes 516104 | tf_op jit(solution)/shard_map/ppermute | solution.py:287
  10.7 9.0 %collective-permute-done.1.a = f32[336,256]{1,0:T(8,128)S(1)} collective-permute-done((f32[336,256]{1,0:T(8,128)S(1)}, f32[336,256]{1,0:T(8,128)S(1)}, u32[]{:S(2)}, u32[]{:S(2)}) %collective-permute-start.1) | collective-permute-done | bytes 344096 | tf_op jit(solution)/shard_map/ppermute | solution.py:287
  20.3 1.4 %collective-permute-done.4.d = f32[168,256]{1,0:T(8,128)S(1)} collective-permute-done((f32[168,256]{1,0:T(8,128)S(1)}, f32[168,256]{1,0:T(8,128)S(1)}, u32[]{:S(2)}, u32[]{:S(2)}) %collective-permute-start.4) | collective-permute-done | bytes 172064 | tf_op jit(solution)/shard_map/ppermute | solution.py:287
  21.7 1.0 %shard_map.70 = (f32[336,256]{1,0:T(8,128)S(1)}, f32[168,256]{1,0:T(8,128)S(1)}, f32[4,336,256]{2,1,0:T(8,128)S(1)}, f32[336,256]{1,0:T(8,128)S(1)}) custom-call(f32[336,256]{1,0:T(8,128)S(1)} %get-tuple-element.18.mine_ref, f32[336,256]{1,0:T(8,128)S(1)} %collective-permute-done.1.a, f32[336,256]{1,0:T(8,128)S(1)} %collective-permute-done.2.b, ...), custom_call_target="tpu_custom_call" | custom-call | flops 377487360 | bytes 1048576 | tf_op jit(solution)/shard_map/pallas_call | solution.py:273
  22.7 0.5 collective-permute-start.5
  23.2 5.4 %collective-permute-done.5.direct_ref = f32[168,256]{1,0:T(8,128)S(1)} collective-permute-done((f32[168,256]{1,0:T(8,128)S(1)}, f32[168,256]{1,0:T(8,128)S(1)}, u32[]{:S(2)}, u32[]{:S(2)}) %collective-permute-start.5) | collective-permute-done | bytes 172064 | tf_op jit(solution)/shard_map/ppermute | solution.py:287
  28.6 1.0 %collective-permute-start.6 = (f32[168,256]{1,0:T(8,128)S(1)}, f32[168,256]{1,0:T(8,128)S(1)}, u32[]{:S(2)}, u32[]{:S(2)}) collective-permute-start(f32[168,256]{1,0:T(8,128)S(1)} %collective-permute-done.5.direct_ref), channel_id=1, source_target_pairs={{0,1},{1,0},{2,3},{3,2},{4,5},{5,4},{6,7},{7,6},{8,9},{9,8},{10,11... | collective-permute-start | bytes 516104 | tf_op jit(solution)/shard_map/ppermute | solution.py:287
  29.6 1.0 %collective-permute-done.6.swapped_ref = f32[168,256]{1,0:T(8,128)S(1)} collective-permute-done((f32[168,256]{1,0:T(8,128)S(1)}, f32[168,256]{1,0:T(8,128)S(1)}, u32[]{:S(2)}, u32[]{:S(2)}) %collective-permute-start.6) | collective-permute-done | bytes 172064 | tf_op jit(solution)/shard_map/ppermute | solution.py:287
  31.0 4.4 %collective-permute-start.7 = (f32[168,256]{1,0:T(8,128)S(1)}, f32[168,256]{1,0:T(8,128)S(1)}, u32[]{:S(2)}, u32[]{:S(2)}) collective-permute-start(f32[168,256]{1,0:T(8,128)S(1)} %get-tuple-element.23), channel_id=1, source_target_pairs={{0,56},{1,57},{2,58},{3,59},{4,60},{5,61},{6,62},{7,63},{8,16},{9,... | collective-permute-start | bytes 516104 | tf_op jit(solution)/shard_map/ppermute | solution.py:287
  35.5 1.6 %collective-permute-start.8 = (f32[88,256]{1,0:T(8,128)S(1)}, f32[88,256]{1,0:T(8,128)S(1)}, u32[]{:S(2)}, u32[]{:S(2)}) collective-permute-start(f32[88,256]{1,0:T(8,128)S(1)} %get-tuple-element.24), channel_id=1, source_target_pairs={{0,40},{1,41},{2,42},{3,43},{4,44},{5,45},{6,46},{7,47},{8,32},{9,... | collective-permute-start | bytes 270344 | tf_op jit(solution)/shard_map/ppermute | solution.py:287
  37.1 3.5 %collective-permute-done.7 = f32[168,256]{1,0:T(8,128)S(1)} collective-permute-done((f32[168,256]{1,0:T(8,128)S(1)}, f32[168,256]{1,0:T(8,128)S(1)}, u32[]{:S(2)}, u32[]{:S(2)}) %collective-permute-start.7) | collective-permute-done | bytes 172064 | tf_op jit(solution)/shard_map/ppermute | solution.py:287
  40.7 2.5 %collective-permute-done.8 = f32[88,256]{1,0:T(8,128)S(1)} collective-permute-done((f32[88,256]{1,0:T(8,128)S(1)}, f32[88,256]{1,0:T(8,128)S(1)}, u32[]{:S(2)}, u32[]{:S(2)}) %collective-permute-start.8) | collective-permute-done | bytes 90144 | tf_op jit(solution)/shard_map/ppermute | solution.py:287
  43.2 0.7 %collective-permute-start.9 = (f32[256,256]{1,0:T(8,128)S(1)}, f32[256,256]{1,0:T(8,128)S(1)}, u32[]{:S(2)}, u32[]{:S(2)}) collective-permute-start(f32[256,256]{1,0:T(8,128)S(1)} %constant_dynamic-update-slice_fusion.a), channel_id=1, source_target_pairs={{0,8},{1,9},{2,10},{3,11},{4,12},{5,13},{6,14},{7,15},{8,0},{9,1},... | collective-permute-start | bytes 786440 | tf_op jit(solution)/shard_map/ppermute | solution.py:287
  43.9 2.8 %collective-permute-start.10 = (f32[256,256]{1,0:T(8,128)S(1)}, f32[256,256]{1,0:T(8,128)S(1)}, u32[]{:S(2)}, u32[]{:S(2)}) collective-permute-start(f32[256,256]{1,0:T(8,128)S(1)} %constant_dynamic-update-slice_fusion.a), channel_id=1, source_target_pairs={{0,1},{1,0},{2,3},{3,2},{4,5},{5,4},{6,7},{7,6},{8,9},{9,8},{10,11... | collective-permute-start | bytes 786440 | tf_op jit(solution)/shard_map/ppermute | solution.py:287
  46.7 3.1 %collective-permute-done.9.b = f32[256,256]{1,0:T(8,128)S(1)} collective-permute-done((f32[256,256]{1,0:T(8,128)S(1)}, f32[256,256]{1,0:T(8,128)S(1)}, u32[]{:S(2)}, u32[]{:S(2)}) %collective-permute-start.9) | collective-permute-done | bytes 262176 | tf_op jit(solution)/shard_map/ppermute | solution.py:287
  49.7 2.3 %collective-permute-start.11 = (f32[256,256]{1,0:T(8,128)S(1)}, f32[256,256]{1,0:T(8,128)S(1)}, u32[]{:S(2)}, u32[]{:S(2)}) collective-permute-start(f32[256,256]{1,0:T(8,128)S(1)} %collective-permute-done.9.b), channel_id=1, source_target_pairs={{0,1},{1,0},{2,3},{3,2},{4,5},{5,4},{6,7},{7,6},{8,9},{9,8},{10,11... | collective-permute-start | bytes 786440 | tf_op jit(solution)/shard_map/ppermute | solution.py:287
  52.0 1.2 %collective-permute-done.11.d = f32[256,256]{1,0:T(8,128)S(1)} collective-permute-done((f32[256,256]{1,0:T(8,128)S(1)}, f32[256,256]{1,0:T(8,128)S(1)}, u32[]{:S(2)}, u32[]{:S(2)}) %collective-permute-start.11) | collective-permute-done | bytes 262176 | tf_op jit(solution)/shard_map/ppermute | solution.py:287
  53.1 1.0 %shard_map.72 = (f32[336,256]{1,0:T(8,128)S(1)}, f32[168,256]{1,0:T(8,128)S(1)}, f32[4,336,256]{2,1,0:T(8,128)S(1)}, f32[336,256]{1,0:T(8,128)S(1)}) custom-call(f32[336,256]{1,0:T(8,128)S(1)} %get-tuple-element.22.mine_ref, f32[256,256]{1,0:T(8,128)S(1)} %constant_dynamic-update-slice_fusion.a, f32[256,256]{1,0:T(8,128)S(1)} %collective-permute-done.9.b, ...), custom_call_target="tpu_custom_call" | custom-call | flops 377487360 | bytes 1048576 | tf_op jit(solution)/shard_map/pallas_call | solution.py:273
  54.1 1.4 %collective-permute-start.12 = (f32[336,256]{1,0:T(8,128)S(1)}, f32[336,256]{1,0:T(8,128)S(1)}, u32[]{:S(2)}, u32[]{:S(2)}) collective-permute-start(f32[336,256]{1,0:T(8,128)S(1)} %get-tuple-element.25.mine_ref), channel_id=1, source_target_pairs={{0,192},{1,65},{2,194},{3,67},{4,196},{5,69},{6,198},{7,71},{8,200... | collective-permute-start | bytes 1032200 | tf_op jit(solution)/shard_map/ppermute | solution.py:287
  55.5 2.6 %collective-permute-start.14 = (f32[168,256]{1,0:T(8,128)S(1)}, f32[168,256]{1,0:T(8,128)S(1)}, u32[]{:S(2)}, u32[]{:S(2)}) collective-permute-start(f32[168,256]{1,0:T(8,128)S(1)} %get-tuple-element.26), channel_id=1, source_target_pairs={{0,128},{1,129},{2,130},{3,131},{4,132},{5,133},{6,134},{7,135},{8... | collective-permute-start | bytes 516104 | tf_op jit(solution)/shard_map/ppermute | solution.py:287
  58.1 3.5 %collective-permute-done.12.a = f32[336,256]{1,0:T(8,128)S(1)} collective-permute-done((f32[336,256]{1,0:T(8,128)S(1)}, f32[336,256]{1,0:T(8,128)S(1)}, u32[]{:S(2)}, u32[]{:S(2)}) %collective-permute-start.12) | collective-permute-done | bytes 344096 | tf_op jit(solution)/shard_map/ppermute | solution.py:287
  61.6 4.2 %collective-permute-start.13 = (f32[336,256]{1,0:T(8,128)S(1)}, f32[336,256]{1,0:T(8,128)S(1)}, u32[]{:S(2)}, u32[]{:S(2)}) collective-permute-start(f32[336,256]{1,0:T(8,128)S(1)} %collective-permute-done.12.a), channel_id=1, source_target_pairs={{0,1},{1,0},{2,3},{3,2},{4,5},{5,4},{6,7},{7,6},{8,9},{9,8},{10,11... | collective-permute-start | bytes 1032200 | tf_op jit(solution)/shard_map/ppermute | solution.py:287
  65.8 0.6 collective-permute-done.14.c
  66.6 0.8 %shard_map.74.w_ref = f32[528,256]{1,0:T(8,128)S(1)} custom-call(f32[528,256]{1,0:T(8,128)S(1)} %shard_map.73.w_ref, f32[4,336,256]{2,1,0:T(8,128)S(1)} %get-tuple-element.27.slots_ref, f32[336,256]{1,0:T(8,128)S(1)} %get-tuple-element.28.tb_ref), custom_call_target="tpu_custom_call" | custom-call | flops 251658240 | bytes 1048576 | tf_op jit(solution)/shard_map/pallas_call | solution.py:273
  67.8 0.8 %shard_map.76.w_ref = f32[528,256]{1,0:T(8,128)S(1)} custom-call(f32[528,256]{1,0:T(8,128)S(1)} %shard_map.75.w_ref, f32[4,336,256]{2,1,0:T(8,128)S(1)} %get-tuple-element.30.slots_ref, f32[336,256]{1,0:T(8,128)S(1)} %get-tuple-element.31.tb_ref), custom_call_target="tpu_custom_call" | custom-call | flops 251658240 | bytes 1048576 | tf_op jit(solution)/shard_map/pallas_call | solution.py:273
  68.7 1.3 %shard_map.77 = (f32[2,256]{1,0:T(2,128)}, f32[1,64]{1,0:T(1,128)}) custom-call(f32[336,256]{1,0:T(8,128)S(1)} %get-tuple-element.25.mine_ref, f32[336,256]{1,0:T(8,128)S(1)} %collective-permute-done.12.a, f32[336,256]{1,0:T(8,128)S(1)} %collective-permute-done.13.b, f32[168,256]{1,0:T(8,128)S(1)} %collective-permute-done.14.c, ...), custom_call_target="tpu_custom_call" | custom-call | flops 125829120 | bytes 1048576 | tf_op jit(solution)/shard_map/pallas_call | solution.py:273
  (22 shorter events, 2.0 us)
Async XLA Ops:
  2.1 1.0 %copy-start = (f32[2,256,256]{2,1,0:T(8,128)S(1)}, f32[2,256,256]{2,1,0:T(8,128)}, u32[]{:S(2)}) copy-start(f32[2,256,256]{2,1,0:T(8,128)} %a_ref.3) | copy-start | bytes 1572868
  3.7 4.6 %collective-permute-start = (f32[336,256]{1,0:T(8,128)S(1)}, f32[336,256]{1,0:T(8,128)S(1)}, u32[]{:S(2)}, u32[]{:S(2)}) collective-permute-start(f32[336,256]{1,0:T(8,128)S(1)} %shard_map.68.mine_ref.t_ref), channel_id=1, source_target_pairs={{0,1},{1,0},{2,3},{3,2},{4,5},{5,4},{6,7},{7,6},{8,9},{9,8},{10,11... | collective-permute-start | bytes 1032200 | tf_op jit(solution)/shard_map/ppermute | solution.py:287
  8.7 11.1 %collective-permute-start.1 = (f32[336,256]{1,0:T(8,128)S(1)}, f32[336,256]{1,0:T(8,128)S(1)}, u32[]{:S(2)}, u32[]{:S(2)}) collective-permute-start(f32[336,256]{1,0:T(8,128)S(1)} %get-tuple-element.18.mine_ref), channel_id=1, source_target_pairs={{0,6},{1,3},{2,0},{3,5},{4,2},{5,7},{6,4},{7,1},{8,14},{9,11},{10,... | collective-permute-start | bytes 1032200 | tf_op jit(solution)/shard_map/ppermute | solution.py:287
  8.8 11.0 %collective-permute-start.3 = (f32[168,256]{1,0:T(8,128)S(1)}, f32[168,256]{1,0:T(8,128)S(1)}, u32[]{:S(2)}, u32[]{:S(2)}) collective-permute-start(f32[168,256]{1,0:T(8,128)S(1)} %get-tuple-element.19), channel_id=1, source_target_pairs={{0,4},{1,5},{2,6},{3,7},{4,0},{5,1},{6,2},{7,3},{8,12},{9,13},{10,... | collective-permute-start | bytes 516104 | tf_op jit(solution)/shard_map/ppermute | solution.py:287
  19.8 1.9 %collective-permute-start.2 = (f32[336,256]{1,0:T(8,128)S(1)}, f32[336,256]{1,0:T(8,128)S(1)}, u32[]{:S(2)}, u32[]{:S(2)}) collective-permute-start(f32[336,256]{1,0:T(8,128)S(1)} %collective-permute-done.1.a), channel_id=1, source_target_pairs={{0,1},{1,0},{2,3},{3,2},{4,5},{5,4},{6,7},{7,6},{8,9},{9,8},{10,11... | collective-permute-start | bytes 1032200 | tf_op jit(solution)/shard_map/ppermute | solution.py:287
  19.8 1.9 %collective-permute-start.4 = (f32[168,256]{1,0:T(8,128)S(1)}, f32[168,256]{1,0:T(8,128)S(1)}, u32[]{:S(2)}, u32[]{:S(2)}) collective-permute-start(f32[168,256]{1,0:T(8,128)S(1)} %collective-permute-done.3.c), channel_id=1, source_target_pairs={{0,1},{1,0},{2,3},{3,2},{4,5},{5,4},{6,7},{7,6},{8,9},{9,8},{10,11... | collective-permute-start | bytes 516104 | tf_op jit(solution)/shard_map/ppermute | solution.py:287
  22.7 43.8 %copy-start.1 = (f32[2,256,256]{2,1,0:T(8,128)S(1)}, f32[2,256,256]{2,1,0:T(8,128)}, u32[]{:S(2)}) copy-start(f32[2,256,256]{2,1,0:T(8,128)} %a_ref.3) | copy-start | bytes 1572868
  22.7 5.9 %collective-permute-start.5 = (f32[168,256]{1,0:T(8,128)S(1)}, f32[168,256]{1,0:T(8,128)S(1)}, u32[]{:S(2)}, u32[]{:S(2)}) collective-permute-start(f32[168,256]{1,0:T(8,128)S(1)} %get-tuple-element.21), channel_id=1, source_target_pairs={{0,8},{1,9},{2,10},{3,11},{4,12},{5,13},{6,14},{7,15},{8,0},{9,1},... | collective-permute-start | bytes 516104 | tf_op jit(solution)/shard_map/ppermute | solution.py:287
  28.6 2.0 %collective-permute-start.6 = (f32[168,256]{1,0:T(8,128)S(1)}, f32[168,256]{1,0:T(8,128)S(1)}, u32[]{:S(2)}, u32[]{:S(2)}) collective-permute-start(f32[168,256]{1,0:T(8,128)S(1)} %collective-permute-done.5.direct_ref), channel_id=1, source_target_pairs={{0,1},{1,0},{2,3},{3,2},{4,5},{5,4},{6,7},{7,6},{8,9},{9,8},{10,11... | collective-permute-start | bytes 516104 | tf_op jit(solution)/shard_map/ppermute | solution.py:287
  31.0 9.6 %collective-permute-start.7 = (f32[168,256]{1,0:T(8,128)S(1)}, f32[168,256]{1,0:T(8,128)S(1)}, u32[]{:S(2)}, u32[]{:S(2)}) collective-permute-start(f32[168,256]{1,0:T(8,128)S(1)} %get-tuple-element.23), channel_id=1, source_target_pairs={{0,56},{1,57},{2,58},{3,59},{4,60},{5,61},{6,62},{7,63},{8,16},{9,... | collective-permute-start | bytes 516104 | tf_op jit(solution)/shard_map/ppermute | solution.py:287
  35.5 7.7 %collective-permute-start.8 = (f32[88,256]{1,0:T(8,128)S(1)}, f32[88,256]{1,0:T(8,128)S(1)}, u32[]{:S(2)}, u32[]{:S(2)}) collective-permute-start(f32[88,256]{1,0:T(8,128)S(1)} %get-tuple-element.24), channel_id=1, source_target_pairs={{0,40},{1,41},{2,42},{3,43},{4,44},{5,45},{6,46},{7,47},{8,32},{9,... | collective-permute-start | bytes 270344 | tf_op jit(solution)/shard_map/ppermute | solution.py:287
  43.2 6.6 %collective-permute-start.9 = (f32[256,256]{1,0:T(8,128)S(1)}, f32[256,256]{1,0:T(8,128)S(1)}, u32[]{:S(2)}, u32[]{:S(2)}) collective-permute-start(f32[256,256]{1,0:T(8,128)S(1)} %constant_dynamic-update-slice_fusion.a), channel_id=1, source_target_pairs={{0,8},{1,9},{2,10},{3,11},{4,12},{5,13},{6,14},{7,15},{8,0},{9,1},... | collective-permute-start | bytes 786440 | tf_op jit(solution)/shard_map/ppermute | solution.py:287
  43.9 8.1 %collective-permute-start.10 = (f32[256,256]{1,0:T(8,128)S(1)}, f32[256,256]{1,0:T(8,128)S(1)}, u32[]{:S(2)}, u32[]{:S(2)}) collective-permute-start(f32[256,256]{1,0:T(8,128)S(1)} %constant_dynamic-update-slice_fusion.a), channel_id=1, source_target_pairs={{0,1},{1,0},{2,3},{3,2},{4,5},{5,4},{6,7},{7,6},{8,9},{9,8},{10,11... | collective-permute-start | bytes 786440 | tf_op jit(solution)/shard_map/ppermute | solution.py:287
  49.7 3.4 %collective-permute-start.11 = (f32[256,256]{1,0:T(8,128)S(1)}, f32[256,256]{1,0:T(8,128)S(1)}, u32[]{:S(2)}, u32[]{:S(2)}) collective-permute-start(f32[256,256]{1,0:T(8,128)S(1)} %collective-permute-done.9.b), channel_id=1, source_target_pairs={{0,1},{1,0},{2,3},{3,2},{4,5},{5,4},{6,7},{7,6},{8,9},{9,8},{10,11... | collective-permute-start | bytes 786440 | tf_op jit(solution)/shard_map/ppermute | solution.py:287
  54.1 7.5 %collective-permute-start.12 = (f32[336,256]{1,0:T(8,128)S(1)}, f32[336,256]{1,0:T(8,128)S(1)}, u32[]{:S(2)}, u32[]{:S(2)}) collective-permute-start(f32[336,256]{1,0:T(8,128)S(1)} %get-tuple-element.25.mine_ref), channel_id=1, source_target_pairs={{0,192},{1,65},{2,194},{3,67},{4,196},{5,69},{6,198},{7,71},{8,200... | collective-permute-start | bytes 1032200 | tf_op jit(solution)/shard_map/ppermute | solution.py:287
  55.5 10.9 %collective-permute-start.14 = (f32[168,256]{1,0:T(8,128)S(1)}, f32[168,256]{1,0:T(8,128)S(1)}, u32[]{:S(2)}, u32[]{:S(2)}) collective-permute-start(f32[168,256]{1,0:T(8,128)S(1)} %get-tuple-element.26), channel_id=1, source_target_pairs={{0,128},{1,129},{2,130},{3,131},{4,132},{5,133},{6,134},{7,135},{8... | collective-permute-start | bytes 516104 | tf_op jit(solution)/shard_map/ppermute | solution.py:287
  61.6 7.0 %collective-permute-start.13 = (f32[336,256]{1,0:T(8,128)S(1)}, f32[336,256]{1,0:T(8,128)S(1)}, u32[]{:S(2)}, u32[]{:S(2)}) collective-permute-start(f32[336,256]{1,0:T(8,128)S(1)} %collective-permute-done.12.a), channel_id=1, source_target_pairs={{0,1},{1,0},{2,3},{3,2},{4,5},{5,4},{6,7},{7,6},{8,9},{9,8},{10,11... | collective-permute-start | bytes 1032200 | tf_op jit(solution)/shard_map/ppermute | solution.py:287
  66.5 2.2 %collective-permute-start.15 = (f32[168,256]{1,0:T(8,128)S(1)}, f32[168,256]{1,0:T(8,128)S(1)}, u32[]{:S(2)}, u32[]{:S(2)}) collective-permute-start(f32[168,256]{1,0:T(8,128)S(1)} %collective-permute-done.14.c), channel_id=1, source_target_pairs={{0,1},{1,0},{2,3},{3,2},{4,5},{5,4},{6,7},{7,6},{8,9},{9,8},{10,11... | collective-permute-start | bytes 516104 | tf_op jit(solution)/shard_map/ppermute | solution.py:287
  67.8 0.9 %copy-start.2 = (f32[256]{0:T(256)S(1)}, f32[256]{0:T(256)}, u32[]{:S(2)}) copy-start(f32[256]{0:T(256)} %param.7) | copy-start | bytes 3076

commit v4 on v2

--- a/solution.py
+++ b/solution.py
@@ -48,10 +48,8 @@
     pairs(lambda y, z, x, c: (y + 2, z, x, c)),
 )
 Z_ONE = pairs(lambda y, z, x, c: (y, z ^ 1, x, c))
-Z_FROM = (
-    pairs(lambda y, z, x, c: (y, z + (2 if c else -2), x, c)),
-    pairs(lambda y, z, x, c: (y, z ^ 5, x, c)),
-)
+Z_SIDE = pairs(lambda y, z, x, c: (y, z + (1 if z % 2 else -1), x, c))
+Z_FAR = pairs(lambda y, z, x, c: (y, z ^ 5, x, c))
 
 
 def split(value):
@@ -150,6 +148,21 @@
     store_half(half_ref, t_ref, core)
 
 
+def fill_z(slots_ref, z, core, mine_ref, far_ref, other_far_ref, *sides):
+    at, odd = lax.div(z, 2), lax.rem(z, 2)
+    slots_ref[at] = mine_ref[...]
+    first = pl.ds(pl.multiple_of(core * HALF, 8), HALF)
+    second = pl.ds(pl.multiple_of((1 - core) * HALF, 8), HALF)
+    far = lax.rem(at + 2, 4)
+    slots_ref[far, first, :] = far_ref[...]
+    slots_ref[far, second, :] = other_far_ref[...]
+    own, got = lax.rem(at + 3 - 2 * odd, 4), lax.rem(at + 1 + 2 * odd, 4)
+    slots_ref[own, first, :] = sides[0][...]
+    slots_ref[own, second, :] = sides[1][...]
+    slots_ref[got, first, :] = sides[2][...]
+    slots_ref[got, second, :] = sides[3][...]
+
+
 def fill(slots_ref, at, core, mine_ref, side_ref, other_side_ref, far_ref, other_far_ref):
     slots_ref[at] = mine_ref[...]
     slots_ref[lax.rem(at + 1 + 2 * core, 4)] = side_ref[...]
@@ -163,9 +176,13 @@
     return x if axis == "x" else lax.div(z, 2)
 
 
-def quad_kernel(axis, mine_ref, a, b, c, d, t_ref, half_ref, slots_ref, tb_ref):
+def quad_kernel(axis, *refs):
+    mine_ref, parts, (t_ref, half_ref, slots_ref, tb_ref) = refs[0], refs[1:-4], refs[-4:]
     _, z, x, core = me()
-    fill(slots_ref, quad_at(axis, z, x), core, mine_ref, a, b, c, d)
+    if axis == "x":
+        fill(slots_ref, x, core, mine_ref, *parts)
+    else:
+        fill_z(slots_ref, z, core, mine_ref, *parts)
     tb = compose(load(slots_ref.at[2]), load(slots_ref.at[3]))
     ta = compose(load(slots_ref.at[0]), load(slots_ref.at[1]))
     store(tb_ref, tb)
@@ -293,7 +310,11 @@
     (own,) = call(part(own_quad_kernel, "x"), [w], [own, slots, tb], products=2)
     total, half, late = call(pair_kernel, [t, h, t], [total, direct, swapped])
 
-    parts = gather(total, half, Z_FROM)
+    side, far = send(half, Z_SIDE), send(half, Z_FAR)
+    got = send(side, Z_ONE)
+    parts = [far, send(far, OTHER_CORE)]
+    for part_ in (side, got):
+        parts += [part_, send(part_, OTHER_CORE)]
     (own,) = call(own_pair_kernel, [w], [own, late])
     total, half, slots, tb = call(
         part(quad_kernel, "z"), [t, h, (4,) + t, t], [total, *parts], products=3

time: 70.6 us -> 67.9 us (0.962)
  starting transfers between devices: 31.7 us -> 28.1 us
  waiting for transfers between devices: 28.4 us -> 29.5 us
    ppermute x15 -> x17, starting transfers between devices: 31.7 us -> 28.1 us  [send(): return lax.ppermute(value, 'tm', move)]
    ppermute x15 -> x17, waiting for transfers between devices: 28.4 us -> 29.5 us  [send(): return lax.ppermute(value, 'tm', move)]
  transfers between devices with their start and end apart: 15 -> 17, of which waited for: 10 -> 10; matrix products, arithmetic and copies ran while one was open for 0% -> 0% of each run, Pallas kernels for 3% -> 3%
where the time goes in v4:
time: 67.9 us; the launch traced here: 67.7 us
  waiting for transfers between devices  29.5 us (43%)
  starting transfers between devices  28.1 us (41%)
  Pallas kernels  6.77 us (10%)
  other arithmetic  1.43 us (2%)
  local copies, waits for them, and re-layouts  1.13 us (2%)
  between operations  0.75 us (1%)
    ppermute x17, waiting for transfers between devices, send(): return lax.ppermute(value, 'tm', move)  29.5 us
    ppermute x17, starting transfers between devices, send(): return lax.ppermute(value, 'tm', move)  28.1 us
    pallas_call x10, Pallas kernels, call(): pl.pallas_call(kernel, out_shape=shapes, in_specs=[VM] * len(args), out_s...  6.77 us
  transfers between devices with their start and end apart: 17, of which 10 were waited for; matrix products, arithmetic and copies ran while one was open for 0% of the time, Pallas kernels for 3%

profile of v4, /device:TPU:1, one launch (start us, length us, event | category | flops | bytes accessed | tf_op | source)
XLA Modules:
  0.0 67.7 jit_solution(1415562940037827696)
XLA Ops:
  0.6 0.7 convert_bitcast_fusion
  1.4 0.8 %fusion.row_ref = f32[8,256]{1,0:T(8,128)S(1)} fusion(f32[1,64]{1,0:T(1,128)S(1)} %convert_bitcast_fusion, f32[2,64]{1,0:T(2,128)} %param.8, f32[2,256]{1,0:T(2,128)} %param.6, f32[8]{0:T(128)S(1)} %pad.13.clone), kind=kLoop, calls=%fused_computation.5 | loop fusion | flops 22528 | bytes 11040 | tf_op jit(solution)/shard_map/concatenate | solution.py:294
  2.1 1.0 %copy-done = f32[2,256,256]{2,1,0:T(8,128)S(1)} copy-done((f32[2,256,256]{2,1,0:T(8,128)S(1)}, f32[2,256,256]{2,1,0:T(8,128)}, u32[]{:S(2)}) %copy-start) | copy-done | bytes 524312
  3.2 0.6 shard_map.68.mine_ref.t_ref
  3.7 3.3 %collective-permute-start = (f32[336,256]{1,0:T(8,128)S(1)}, f32[336,256]{1,0:T(8,128)S(1)}, u32[]{:S(2)}, u32[]{:S(2)}) collective-permute-start(f32[336,256]{1,0:T(8,128)S(1)} %shard_map.68.mine_ref.t_ref), channel_id=1, source_target_pairs={{0,1},{1,0},{2,3},{3,2},{4,5},{5,4},{6,7},{7,6},{8,9},{9,8},{10,11... | collective-permute-start | bytes 1032200 | tf_op jit(solution)/shard_map/ppermute | solution.py:282
  7.0 1.3 %collective-permute-done.other_ref = f32[336,256]{1,0:T(8,128)S(1)} collective-permute-done((f32[336,256]{1,0:T(8,128)S(1)}, f32[336,256]{1,0:T(8,128)S(1)}, u32[]{:S(2)}, u32[]{:S(2)}) %collective-permute-start) | collective-permute-done | bytes 344096 | tf_op jit(solution)/shard_map/ppermute | solution.py:282
  8.8 1.9 %collective-permute-start.3 = (f32[168,256]{1,0:T(8,128)S(1)}, f32[168,256]{1,0:T(8,128)S(1)}, u32[]{:S(2)}, u32[]{:S(2)}) collective-permute-start(f32[168,256]{1,0:T(8,128)S(1)} %get-tuple-element.18), channel_id=1, source_target_pairs={{0,4},{1,5},{2,6},{3,7},{4,0},{5,1},{6,2},{7,3},{8,12},{9,13},{10,... | collective-permute-start | bytes 516104 | tf_op jit(solution)/shard_map/ppermute | solution.py:282
  10.7 9.0 %collective-permute-done.1.refs_1_ = f32[336,256]{1,0:T(8,128)S(1)} collective-permute-done((f32[336,256]{1,0:T(8,128)S(1)}, f32[336,256]{1,0:T(8,128)S(1)}, u32[]{:S(2)}, u32[]{:S(2)}) %collective-permute-start.1) | collective-permute-done | bytes 344096 | tf_op jit(solution)/shard_map/ppermute | solution.py:282
  19.8 0.5 collective-permute-start.4
  20.3 1.4 %collective-permute-done.4.refs_4_ = f32[168,256]{1,0:T(8,128)S(1)} collective-permute-done((f32[168,256]{1,0:T(8,128)S(1)}, f32[168,256]{1,0:T(8,128)S(1)}, u32[]{:S(2)}, u32[]{:S(2)}) %collective-permute-start.4) | collective-permute-done | bytes 172064 | tf_op jit(solution)/shard_map/ppermute | solution.py:282
  21.7 1.0 %shard_map.70 = (f32[336,256]{1,0:T(8,128)S(1)}, f32[168,256]{1,0:T(8,128)S(1)}, f32[4,336,256]{2,1,0:T(8,128)S(1)}, f32[336,256]{1,0:T(8,128)S(1)}) custom-call(f32[336,256]{1,0:T(8,128)S(1)} %get-tuple-element.17.refs_0_, f32[336,256]{1,0:T(8,128)S(1)} %collective-permute-done.1.refs_1_, f32[336,256]{1,0:T(8,128)S(1)} %collective-permute-done.2.refs_2_, ...), custom_call_target="tpu_custom_call" | custom-call | flops 377487360 | bytes 1048576 | tf_op jit(solution)/shard_map/pallas_call | solution.py:268
  22.7 0.5 collective-permute-start.5
  23.2 5.4 %collective-permute-done.5.direct_ref = f32[168,256]{1,0:T(8,128)S(1)} collective-permute-done((f32[168,256]{1,0:T(8,128)S(1)}, f32[168,256]{1,0:T(8,128)S(1)}, u32[]{:S(2)}, u32[]{:S(2)}) %collective-permute-start.5) | collective-permute-done | bytes 172064 | tf_op jit(solution)/shard_map/ppermute | solution.py:282
  28.6 1.0 %collective-permute-start.6 = (f32[168,256]{1,0:T(8,128)S(1)}, f32[168,256]{1,0:T(8,128)S(1)}, u32[]{:S(2)}, u32[]{:S(2)}) collective-permute-start(f32[168,256]{1,0:T(8,128)S(1)} %collective-permute-done.5.direct_ref), channel_id=1, source_target_pairs={{0,1},{1,0},{2,3},{3,2},{4,5},{5,4},{6,7},{7,6},{8,9},{9,8},{10,11... | collective-permute-start | bytes 516104 | tf_op jit(solution)/shard_map/ppermute | solution.py:282
  29.6 1.0 %collective-permute-done.6.swapped_ref = f32[168,256]{1,0:T(8,128)S(1)} collective-permute-done((f32[168,256]{1,0:T(8,128)S(1)}, f32[168,256]{1,0:T(8,128)S(1)}, u32[]{:S(2)}, u32[]{:S(2)}) %collective-permute-start.6) | collective-permute-done | bytes 172064 | tf_op jit(solution)/shard_map/ppermute | solution.py:282
  31.0 4.4 %collective-permute-start.9 = (f32[168,256]{1,0:T(8,128)S(1)}, f32[168,256]{1,0:T(8,128)S(1)}, u32[]{:S(2)}, u32[]{:S(2)}) collective-permute-start(f32[168,256]{1,0:T(8,128)S(1)} %get-tuple-element.22), channel_id=1, source_target_pairs={{0,56},{1,57},{2,58},{3,59},{4,60},{5,61},{6,62},{7,63},{8,16},{9,... | collective-permute-start | bytes 516104 | tf_op jit(solution)/shard_map/ppermute | solution.py:282
  35.5 1.6 %collective-permute-start.7 = (f32[168,256]{1,0:T(8,128)S(1)}, f32[168,256]{1,0:T(8,128)S(1)}, u32[]{:S(2)}, u32[]{:S(2)}) collective-permute-start(f32[168,256]{1,0:T(8,128)S(1)} %get-tuple-element.22), channel_id=1, source_target_pairs={{0,40},{1,41},{2,42},{3,43},{4,44},{5,45},{6,46},{7,47},{8,32},{9,... | collective-permute-start | bytes 516104 | tf_op jit(solution)/shard_map/ppermute | solution.py:282
  37.1 4.4 %collective-permute-done.9.refs_3_ = f32[168,256]{1,0:T(8,128)S(1)} collective-permute-done((f32[168,256]{1,0:T(8,128)S(1)}, f32[168,256]{1,0:T(8,128)S(1)}, u32[]{:S(2)}, u32[]{:S(2)}) %collective-permute-start.9) | collective-permute-done | bytes 172064 | tf_op jit(solution)/shard_map/ppermute | solution.py:282
  41.5 2.9 %collective-permute-start.10 = (f32[168,256]{1,0:T(8,128)S(1)}, f32[168,256]{1,0:T(8,128)S(1)}, u32[]{:S(2)}, u32[]{:S(2)}) collective-permute-start(f32[168,256]{1,0:T(8,128)S(1)} %collective-permute-done.9.refs_3_), channel_id=1, source_target_pairs={{0,1},{1,0},{2,3},{3,2},{4,5},{5,4},{6,7},{7,6},{8,9},{9,8},{10,11... | collective-permute-start | bytes 516104 | tf_op jit(solution)/shard_map/ppermute | solution.py:282
  44.4 1.8 %collective-permute-done.7.refs_1_ = f32[168,256]{1,0:T(8,128)S(1)} collective-permute-done((f32[168,256]{1,0:T(8,128)S(1)}, f32[168,256]{1,0:T(8,128)S(1)}, u32[]{:S(2)}, u32[]{:S(2)}) %collective-permute-start.7) | collective-permute-done | bytes 172064 | tf_op jit(solution)/shard_map/ppermute | solution.py:282
  46.2 1.3 %collective-permute-start.8 = (f32[168,256]{1,0:T(8,128)S(1)}, f32[168,256]{1,0:T(8,128)S(1)}, u32[]{:S(2)}, u32[]{:S(2)}) collective-permute-start(f32[168,256]{1,0:T(8,128)S(1)} %collective-permute-done.7.refs_1_), channel_id=1, source_target_pairs={{0,1},{1,0},{2,3},{3,2},{4,5},{5,4},{6,7},{7,6},{8,9},{9,8},{10,11... | collective-permute-start | bytes 516104 | tf_op jit(solution)/shard_map/ppermute | solution.py:282
  47.5 2.3 %collective-permute-start.12 = (f32[168,256]{1,0:T(8,128)S(1)}, f32[168,256]{1,0:T(8,128)S(1)}, u32[]{:S(2)}, u32[]{:S(2)}) collective-permute-start(f32[168,256]{1,0:T(8,128)S(1)} %collective-permute-done.11.refs_5_), channel_id=1, source_target_pairs={{0,1},{1,0},{2,3},{3,2},{4,5},{5,4},{6,7},{7,6},{8,9},{9,8},{10,11... | collective-permute-start | bytes 516104 | tf_op jit(solution)/shard_map/ppermute | solution.py:282
  49.8 1.0 %collective-permute-done.12.refs_6_ = f32[168,256]{1,0:T(8,128)S(1)} collective-permute-done((f32[168,256]{1,0:T(8,128)S(1)}, f32[168,256]{1,0:T(8,128)S(1)}, u32[]{:S(2)}, u32[]{:S(2)}) %collective-permute-start.12) | collective-permute-done | bytes 172064 | tf_op jit(solution)/shard_map/ppermute | solution.py:282
  50.9 1.0 %shard_map.72 = (f32[336,256]{1,0:T(8,128)S(1)}, f32[168,256]{1,0:T(8,128)S(1)}, f32[4,336,256]{2,1,0:T(8,128)S(1)}, f32[336,256]{1,0:T(8,128)S(1)}) custom-call(f32[336,256]{1,0:T(8,128)S(1)} %get-tuple-element.21.refs_0_, f32[168,256]{1,0:T(8,128)S(1)} %collective-permute-done.7.refs_1_, f32[168,256]{1,0:T(8,128)S(1)} %collective-permute-done.8.refs_2_, ...), custom_call_target="tpu_custom_call" | custom-call | flops 377487360 | bytes 1048576 | tf_op jit(solution)/shard_map/pallas_call | solution.py:268
  51.9 1.4 %collective-permute-start.13 = (f32[336,256]{1,0:T(8,128)S(1)}, f32[336,256]{1,0:T(8,128)S(1)}, u32[]{:S(2)}, u32[]{:S(2)}) collective-permute-start(f32[336,256]{1,0:T(8,128)S(1)} %get-tuple-element.23.mine_ref), channel_id=1, source_target_pairs={{0,192},{1,65},{2,194},{3,67},{4,196},{5,69},{6,198},{7,71},{8,200... | collective-permute-start | bytes 1032200 | tf_op jit(solution)/shard_map/ppermute | solution.py:282
  53.2 2.6 %collective-permute-start.15 = (f32[168,256]{1,0:T(8,128)S(1)}, f32[168,256]{1,0:T(8,128)S(1)}, u32[]{:S(2)}, u32[]{:S(2)}) collective-permute-start(f32[168,256]{1,0:T(8,128)S(1)} %get-tuple-element.24), channel_id=1, source_target_pairs={{0,128},{1,129},{2,130},{3,131},{4,132},{5,133},{6,134},{7,135},{8... | collective-permute-start | bytes 516104 | tf_op jit(solution)/shard_map/ppermute | solution.py:282
  55.9 3.5 %collective-permute-done.13.a = f32[336,256]{1,0:T(8,128)S(1)} collective-permute-done((f32[336,256]{1,0:T(8,128)S(1)}, f32[336,256]{1,0:T(8,128)S(1)}, u32[]{:S(2)}, u32[]{:S(2)}) %collective-permute-start.13) | collective-permute-done | bytes 344096 | tf_op jit(solution)/shard_map/ppermute | solution.py:282
  59.3 4.2 %collective-permute-start.14 = (f32[336,256]{1,0:T(8,128)S(1)}, f32[336,256]{1,0:T(8,128)S(1)}, u32[]{:S(2)}, u32[]{:S(2)}) collective-permute-start(f32[336,256]{1,0:T(8,128)S(1)} %collective-permute-done.13.a), channel_id=1, source_target_pairs={{0,1},{1,0},{2,3},{3,2},{4,5},{5,4},{6,7},{7,6},{8,9},{9,8},{10,11... | collective-permute-start | bytes 1032200 | tf_op jit(solution)/shard_map/ppermute | solution.py:282
  63.6 0.6 collective-permute-done.15.c
  64.3 0.8 %shard_map.74.w_ref = f32[528,256]{1,0:T(8,128)S(1)} custom-call(f32[528,256]{1,0:T(8,128)S(1)} %shard_map.73.w_ref, f32[4,336,256]{2,1,0:T(8,128)S(1)} %get-tuple-element.25.slots_ref, f32[336,256]{1,0:T(8,128)S(1)} %get-tuple-element.26.tb_ref), custom_call_target="tpu_custom_call" | custom-call | flops 251658240 | bytes 1048576 | tf_op jit(solution)/shard_map/pallas_call | solution.py:268
  65.5 0.8 %shard_map.76.w_ref = f32[528,256]{1,0:T(8,128)S(1)} custom-call(f32[528,256]{1,0:T(8,128)S(1)} %shard_map.75.w_ref, f32[4,336,256]{2,1,0:T(8,128)S(1)} %get-tuple-element.28.slots_ref, f32[336,256]{1,0:T(8,128)S(1)} %get-tuple-element.29.tb_ref), custom_call_target="tpu_custom_call" | custom-call | flops 251658240 | bytes 1048576 | tf_op jit(solution)/shard_map/pallas_call | solution.py:268
  66.4 1.3 %shard_map.77 = (f32[2,256]{1,0:T(2,128)}, f32[1,64]{1,0:T(1,128)}) custom-call(f32[336,256]{1,0:T(8,128)S(1)} %get-tuple-element.23.mine_ref, f32[336,256]{1,0:T(8,128)S(1)} %collective-permute-done.13.a, f32[336,256]{1,0:T(8,128)S(1)} %collective-permute-done.14.b, f32[168,256]{1,0:T(8,128)S(1)} %collective-permute-done.15.c, ...), custom_call_target="tpu_custom_call" | custom-call | flops 125829120 | bytes 1048576 | tf_op jit(solution)/shard_map/pallas_call | solution.py:268
  (22 shorter events, 1.5 us)
Async XLA Ops:
  2.1 1.0 %copy-start = (f32[2,256,256]{2,1,0:T(8,128)S(1)}, f32[2,256,256]{2,1,0:T(8,128)}, u32[]{:S(2)}) copy-start(f32[2,256,256]{2,1,0:T(8,128)} %a_ref.3) | copy-start | bytes 1572868
  3.7 4.6 %collective-permute-start = (f32[336,256]{1,0:T(8,128)S(1)}, f32[336,256]{1,0:T(8,128)S(1)}, u32[]{:S(2)}, u32[]{:S(2)}) collective-permute-start(f32[336,256]{1,0:T(8,128)S(1)} %shard_map.68.mine_ref.t_ref), channel_id=1, source_target_pairs={{0,1},{1,0},{2,3},{3,2},{4,5},{5,4},{6,7},{7,6},{8,9},{9,8},{10,11... | collective-permute-start | bytes 1032200 | tf_op jit(solution)/shard_map/ppermute | solution.py:282
  8.7 11.1 %collective-permute-start.1 = (f32[336,256]{1,0:T(8,128)S(1)}, f32[336,256]{1,0:T(8,128)S(1)}, u32[]{:S(2)}, u32[]{:S(2)}) collective-permute-start(f32[336,256]{1,0:T(8,128)S(1)} %get-tuple-element.17.refs_0_), channel_id=1, source_target_pairs={{0,6},{1,3},{2,0},{3,5},{4,2},{5,7},{6,4},{7,1},{8,14},{9,11},{10,... | collective-permute-start | bytes 1032200 | tf_op jit(solution)/shard_map/ppermute | solution.py:282
  8.8 11.0 %collective-permute-start.3 = (f32[168,256]{1,0:T(8,128)S(1)}, f32[168,256]{1,0:T(8,128)S(1)}, u32[]{:S(2)}, u32[]{:S(2)}) collective-permute-start(f32[168,256]{1,0:T(8,128)S(1)} %get-tuple-element.18), channel_id=1, source_target_pairs={{0,4},{1,5},{2,6},{3,7},{4,0},{5,1},{6,2},{7,3},{8,12},{9,13},{10,... | collective-permute-start | bytes 516104 | tf_op jit(solution)/shard_map/ppermute | solution.py:282
  19.8 1.9 %collective-permute-start.2 = (f32[336,256]{1,0:T(8,128)S(1)}, f32[336,256]{1,0:T(8,128)S(1)}, u32[]{:S(2)}, u32[]{:S(2)}) collective-permute-start(f32[336,256]{1,0:T(8,128)S(1)} %collective-permute-done.1.refs_1_), channel_id=1, source_target_pairs={{0,1},{1,0},{2,3},{3,2},{4,5},{5,4},{6,7},{7,6},{8,9},{9,8},{10,11... | collective-permute-start | bytes 1032200 | tf_op jit(solution)/shard_map/ppermute | solution.py:282
  19.8 1.9 %collective-permute-start.4 = (f32[168,256]{1,0:T(8,128)S(1)}, f32[168,256]{1,0:T(8,128)S(1)}, u32[]{:S(2)}, u32[]{:S(2)}) collective-permute-start(f32[168,256]{1,0:T(8,128)S(1)} %collective-permute-done.3.refs_3_), channel_id=1, source_target_pairs={{0,1},{1,0},{2,3},{3,2},{4,5},{5,4},{6,7},{7,6},{8,9},{9,8},{10,11... | collective-permute-start | bytes 516104 | tf_op jit(solution)/shard_map/ppermute | solution.py:282
  22.7 41.5 %copy-start.1 = (f32[2,256,256]{2,1,0:T(8,128)S(1)}, f32[2,256,256]{2,1,0:T(8,128)}, u32[]{:S(2)}) copy-start(f32[2,256,256]{2,1,0:T(8,128)} %a_ref.3) | copy-start | bytes 1572868
  22.7 5.9 %collective-permute-start.5 = (f32[168,256]{1,0:T(8,128)S(1)}, f32[168,256]{1,0:T(8,128)S(1)}, u32[]{:S(2)}, u32[]{:S(2)}) collective-permute-start(f32[168,256]{1,0:T(8,128)S(1)} %get-tuple-element.20), channel_id=1, source_target_pairs={{0,8},{1,9},{2,10},{3,11},{4,12},{5,13},{6,14},{7,15},{8,0},{9,1},... | collective-permute-start | bytes 516104 | tf_op jit(solution)/shard_map/ppermute | solution.py:282
  28.6 2.0 %collective-permute-start.6 = (f32[168,256]{1,0:T(8,128)S(1)}, f32[168,256]{1,0:T(8,128)S(1)}, u32[]{:S(2)}, u32[]{:S(2)}) collective-permute-start(f32[168,256]{1,0:T(8,128)S(1)} %collective-permute-done.5.direct_ref), channel_id=1, source_target_pairs={{0,1},{1,0},{2,3},{3,2},{4,5},{5,4},{6,7},{7,6},{8,9},{9,8},{10,11... | collective-permute-start | bytes 516104 | tf_op jit(solution)/shard_map/ppermute | solution.py:282
  31.0 10.5 %collective-permute-start.9 = (f32[168,256]{1,0:T(8,128)S(1)}, f32[168,256]{1,0:T(8,128)S(1)}, u32[]{:S(2)}, u32[]{:S(2)}) collective-permute-start(f32[168,256]{1,0:T(8,128)S(1)} %get-tuple-element.22), channel_id=1, source_target_pairs={{0,56},{1,57},{2,58},{3,59},{4,60},{5,61},{6,62},{7,63},{8,16},{9,... | collective-permute-start | bytes 516104 | tf_op jit(solution)/shard_map/ppermute | solution.py:282
  35.5 10.8 %collective-permute-start.7 = (f32[168,256]{1,0:T(8,128)S(1)}, f32[168,256]{1,0:T(8,128)S(1)}, u32[]{:S(2)}, u32[]{:S(2)}) collective-permute-start(f32[168,256]{1,0:T(8,128)S(1)} %get-tuple-element.22), channel_id=1, source_target_pairs={{0,40},{1,41},{2,42},{3,43},{4,44},{5,45},{6,46},{7,47},{8,32},{9,... | collective-permute-start | bytes 516104 | tf_op jit(solution)/shard_map/ppermute | solution.py:282
  41.5 5.9 %collective-permute-start.11 = (f32[168,256]{1,0:T(8,128)S(1)}, f32[168,256]{1,0:T(8,128)S(1)}, u32[]{:S(2)}, u32[]{:S(2)}) collective-permute-start(f32[168,256]{1,0:T(8,128)S(1)} %collective-permute-done.9.refs_3_), channel_id=1, source_target_pairs={{0,8},{1,9},{2,10},{3,11},{4,12},{5,13},{6,14},{7,15},{8,0},{9,1},... | collective-permute-start | bytes 516104 | tf_op jit(solution)/shard_map/ppermute | solution.py:282
  41.5 8.3 %collective-permute-start.10 = (f32[168,256]{1,0:T(8,128)S(1)}, f32[168,256]{1,0:T(8,128)S(1)}, u32[]{:S(2)}, u32[]{:S(2)}) collective-permute-start(f32[168,256]{1,0:T(8,128)S(1)} %collective-permute-done.9.refs_3_), channel_id=1, source_target_pairs={{0,1},{1,0},{2,3},{3,2},{4,5},{5,4},{6,7},{7,6},{8,9},{9,8},{10,11... | collective-permute-start | bytes 516104 | tf_op jit(solution)/shard_map/ppermute | solution.py:282
  46.2 3.6 %collective-permute-start.8 = (f32[168,256]{1,0:T(8,128)S(1)}, f32[168,256]{1,0:T(8,128)S(1)}, u32[]{:S(2)}, u32[]{:S(2)}) collective-permute-start(f32[168,256]{1,0:T(8,128)S(1)} %collective-permute-done.7.refs_1_), channel_id=1, source_target_pairs={{0,1},{1,0},{2,3},{3,2},{4,5},{5,4},{6,7},{7,6},{8,9},{9,8},{10,11... | collective-permute-start | bytes 516104 | tf_op jit(solution)/shard_map/ppermute | solution.py:282
  47.5 3.4 %collective-permute-start.12 = (f32[168,256]{1,0:T(8,128)S(1)}, f32[168,256]{1,0:T(8,128)S(1)}, u32[]{:S(2)}, u32[]{:S(2)}) collective-permute-start(f32[168,256]{1,0:T(8,128)S(1)} %collective-permute-done.11.refs_5_), channel_id=1, source_target_pairs={{0,1},{1,0},{2,3},{3,2},{4,5},{5,4},{6,7},{7,6},{8,9},{9,8},{10,11... | collective-permute-start | bytes 516104 | tf_op jit(solution)/shard_map/ppermute | solution.py:282
  51.9 7.5 %collective-permute-start.13 = (f32[336,256]{1,0:T(8,128)S(1)}, f32[336,256]{1,0:T(8,128)S(1)}, u32[]{:S(2)}, u32[]{:S(2)}) collective-permute-start(f32[336,256]{1,0:T(8,128)S(1)} %get-tuple-element.23.mine_ref), channel_id=1, source_target_pairs={{0,192},{1,65},{2,194},{3,67},{4,196},{5,69},{6,198},{7,71},{8,200... | collective-permute-start | bytes 1032200 | tf_op jit(solution)/shard_map/ppermute | solution.py:282
  53.2 10.9 %collective-permute-start.15 = (f32[168,256]{1,0:T(8,128)S(1)}, f32[168,256]{1,0:T(8,128)S(1)}, u32[]{:S(2)}, u32[]{:S(2)}) collective-permute-start(f32[168,256]{1,0:T(8,128)S(1)} %get-tuple-element.24), channel_id=1, source_target_pairs={{0,128},{1,129},{2,130},{3,131},{4,132},{5,133},{6,134},{7,135},{8... | collective-permute-start | bytes 516104 | tf_op jit(solution)/shard_map/ppermute | solution.py:282
  59.3 7.0 %collective-permute-start.14 = (f32[336,256]{1,0:T(8,128)S(1)}, f32[336,256]{1,0:T(8,128)S(1)}, u32[]{:S(2)}, u32[]{:S(2)}) collective-permute-start(f32[336,256]{1,0:T(8,128)S(1)} %collective-permute-done.13.a), channel_id=1, source_target_pairs={{0,1},{1,0},{2,3},{3,2},{4,5},{5,4},{6,7},{7,6},{8,9},{9,8},{10,11... | collective-permute-start | bytes 1032200 | tf_op jit(solution)/shard_map/ppermute | solution.py:282
  64.2 2.2 %collective-permute-start.16 = (f32[168,256]{1,0:T(8,128)S(1)}, f32[168,256]{1,0:T(8,128)S(1)}, u32[]{:S(2)}, u32[]{:S(2)}) collective-permute-start(f32[168,256]{1,0:T(8,128)S(1)} %collective-permute-done.15.c), channel_id=1, source_target_pairs={{0,1},{1,0},{2,3},{3,2},{4,5},{5,4},{6,7},{7,6},{8,9},{9,8},{10,11... | collective-permute-start | bytes 516104 | tf_op jit(solution)/shard_map/ppermute | solution.py:282
  65.5 0.9 %copy-start.2 = (f32[256]{0:T(256)S(1)}, f32[256]{0:T(256)}, u32[]{:S(2)}) copy-start(f32[256]{0:T(256)} %param.7) | copy-start | bytes 3076
